TPU v7x, 128 devices: a whole 4x4x4 slice. The times are simulated.
128 devices in a mesh: pb: 16 (over x, z_hi, core), ka: 8 (over y, z_lo).
Axes of the slice: x: 4, y: 4, z: 4 (z_hi: 2, z_lo: 2; z = z_hi * 2 + z_lo), core: 2. Of those that a mesh axis runs over, the one named last changes fastest.
Arguments:
- atoms: bfloat16 [49152, 128], P('pb'), may hold values from -6 to 6
- atom_gain: float32 [128], replicated, may hold values from 0.1 to 1.9
- atom_qkv: bfloat16 [128, 384], replicated, may hold values from -0.5 to 0.5
- atom_proj: bfloat16 [128, 128], replicated, may hold values from -0.5 to 0.5
- atom_bias: bfloat16 [4, 49152, 128], P(None, 'pb'), may hold values from -4 to 250
- window_shift: int32 [1536], P('pb'), may hold values from -64 to -32, as said below
- token_of_atom: int32 [49152], P('pb'), may hold values from 0 to 6143, as said below
- agg_weight: bfloat16 [128, 768], replicated, may hold values from -0.5 to 0.5
- token_gain: float32 [768], replicated, may hold values from 0.1 to 1.9
- token_q: bfloat16 [768, 768], replicated, may hold values from -0.21875 to 0.21875
- token_kv: bfloat16 [768, 1536], replicated, may hold values from -0.21875 to 0.21875
- token_o: bfloat16 [768, 768], replicated, may hold values from -0.21875 to 0.21875
- pair_bias: bfloat16 [16, 6144, 6144], P(None, 'pb', 'ka'), may hold values from -4 to 250
Outputs:
- atom_out: bfloat16 [49152, 128], P('pb')
- tokens_out: bfloat16 [6144, 768], P('pb')
Inputs may be any that keep to these rules, and one draw needn't show every extreme that they name: token_of_atom never falls along the atoms and names every token at least once. Of the 3072 atoms of one index of pb, all but its last ones belong to that index's own 384 tokens; for every index but the final one, its last 192 to 384 atoms belong to the tokens of the index after, and the final index's atoms are all its own. In every draw some index has all of its last 384 atoms in the index after. The key window of query block b begins at atom 32 b + window_shift[b]; both ends of the range occur in every draw.
All inputs are finite; a program needn't handle non-finite values.
Results may differ from a plain program's by a relative error of at most 0.0095.
Values may be sent and summed in bfloat16 or wider, within the bound.
A program may use at most 128 MiB of HBM per device.

v0:
```python
import math

import jax
import jax.numpy as jnp
from jax import lax
from jax.sharding import PartitionSpec as P

AH = 4
TH = 16
WIN_Q = 32
WIN_K = 128
SHIFT_MAX = 384


def extended(cells, sides, width):
    for axis, dim in sides:
        count = lax.axis_size(axis)
        ends = count - 1
        head = lax.slice_in_dim(cells, 0, width, axis=dim)
        tail = lax.slice_in_dim(cells, cells.shape[dim] - width, cells.shape[dim], axis=dim)
        cells = jnp.concatenate(
            [
                lax.ppermute(tail, axis, [(i, (i + 1) % count) for i in range(ends)]),
                cells,
                lax.ppermute(head, axis, [((i + 1) % count, i) for i in range(ends)]),
            ],
            axis=dim,
        )
    return cells


def from_behind(shard, axis, by):
    count = lax.axis_size(axis)
    pairs = [(i, i + by) for i in range(count) if 0 <= i + by < count]
    return lax.ppermute(shard, axis, pairs)


def combined_all(shard, axis, combine):
    everything = jax.tree.map(lambda part: lax.all_gather(part, axis), shard)
    leading = jax.tree.map(lambda part: part[0], everything)

    def hop(k, so_far):
        return combine(so_far, jax.tree.map(lambda part: part[k], everything))

    return lax.fori_loop(1, lax.axis_size(axis), hop, leading)


def layer_norm(values, gain_vec):
    as_float = values.astype(jnp.float32)
    centre = jnp.mean(as_float, axis=-1, keepdims=True)
    spread = jnp.mean(jnp.square(as_float - centre), axis=-1, keepdims=True)
    return (as_float - centre) * lax.rsqrt(spread + 1e-05) * gain_vec


def merge_parts(first_part, second_part):
    top_one, total_one, mixed_one = first_part
    top_two, total_two, mixed_two = second_part
    top_both = jnp.maximum(top_one, top_two)
    scale_one = jnp.exp(top_one - top_both)
    scale_two = jnp.exp(top_two - top_both)
    return (
        top_both,
        total_one * scale_one + total_two * scale_two,
        mixed_one * scale_one[:, :, None] + mixed_two * scale_two[:, :, None],
    )


def body(
    atoms,
    atom_gain,
    atom_qkv,
    atom_proj,
    atom_bias,
    window_shift,
    token_of_atom,
    agg_weight,
    token_gain,
    token_q,
    token_kv,
    token_o,
    pair_bias,
):
    atom_rows, atom_width = atoms.shape
    atom_head = atom_width // AH
    half_win = WIN_K // 2
    shard_index = lax.axis_index("pb")
    atom_total = atom_rows * lax.axis_size("pb")
    normed = layer_norm(atoms, atom_gain).astype(jnp.bfloat16)
    projected = jnp.dot(normed, atom_qkv, preferred_element_type=jnp.float32).astype(jnp.bfloat16)
    padded = extended(projected[:, atom_width:], (("pb", 0),), half_win)
    blocks = atom_rows // WIN_Q
    window_first = jnp.arange(blocks, dtype=jnp.int32) * WIN_Q + window_shift
    key_index = window_first[:, None] + jnp.arange(WIN_K, dtype=jnp.int32)[None, :]
    gathered = jnp.take(padded, key_index + half_win, axis=0)
    global_key = key_index + shard_index * atom_rows
    in_range = (global_key >= 0) & (global_key < atom_total)
    query_heads = projected[:, :atom_width].reshape(blocks, WIN_Q, AH, atom_head)
    key_heads = gathered[:, :, :atom_width].reshape(blocks, WIN_K, AH, atom_head)
    value_heads = gathered[:, :, atom_width:].reshape(blocks, WIN_K, AH, atom_head)
    scores = jnp.einsum(
        "bqhd,bkhd->hbqk", query_heads, key_heads, preferred_element_type=jnp.float32
    ) / math.sqrt(atom_head)
    scores = scores + atom_bias.astype(jnp.float32).reshape(AH, blocks, WIN_Q, WIN_K)
    scores = jnp.where(in_range[None, :, None, :], scores, -jnp.inf)
    exp_terms = jnp.exp(scores - jnp.max(scores, axis=-1, keepdims=True))
    weights = (exp_terms / jnp.sum(exp_terms, axis=-1, keepdims=True)).astype(jnp.bfloat16)
    atom_mixed = jnp.einsum(
        "hbqk,bkhd->bqhd", weights, value_heads, preferred_element_type=jnp.float32
    )
    atom_mixed = atom_mixed.reshape(atom_rows, atom_width).astype(jnp.bfloat16)
    atom_out = (
        atoms.astype(jnp.float32)
        + jnp.dot(atom_mixed, atom_proj, preferred_element_type=jnp.float32)
    ).astype(jnp.bfloat16)
    hidden = jax.nn.silu(jnp.dot(atom_out, agg_weight, preferred_element_type=jnp.float32)).astype(
        jnp.bfloat16
    )
    tok_rows = pair_bias.shape[1]
    slot_ids = jnp.arange(tok_rows, dtype=jnp.int32)[:, None]
    local_token = token_of_atom - shard_index * tok_rows
    own_hot = (local_token[None, :] == slot_ids).astype(jnp.bfloat16)
    own_sum = jnp.dot(own_hot, hidden, preferred_element_type=jnp.float32)
    own_count = jnp.sum(own_hot, axis=1, dtype=jnp.float32)
    edge_rows = SHIFT_MAX
    tail_hot = ((local_token[atom_rows - edge_rows :] - tok_rows)[None, :] == slot_ids).astype(
        jnp.bfloat16
    )
    fore_sum = jnp.dot(
        tail_hot, hidden[atom_rows - edge_rows :], preferred_element_type=jnp.float32
    )
    fore_count = jnp.sum(tail_hot, axis=1, dtype=jnp.float32)
    from_before = (
        from_behind(fore_sum.astype(jnp.bfloat16), "pb", 1).astype(fore_sum.dtype),
        from_behind(fore_count.astype(jnp.bfloat16), "pb", 1).astype(fore_count.dtype),
    )
    token_sums = own_sum + from_before[0]
    token_counts = own_count + from_before[1]
    token_repr = (token_sums / token_counts[:, None]).astype(jnp.bfloat16)
    token_normed = layer_norm(token_repr, token_gain).astype(jnp.bfloat16)
    queries = jnp.dot(token_normed, token_q, preferred_element_type=jnp.float32).astype(
        jnp.bfloat16
    )
    group_ratio = lax.axis_size("pb") // lax.axis_size("ka")
    key_group = lax.axis_index("ka")
    every_row = lax.all_gather(token_normed, "pb", axis=0, tiled=True)
    key_source = lax.dynamic_slice_in_dim(
        every_row, key_group * group_ratio * tok_rows, group_ratio * tok_rows, 0
    )
    keyvals = jnp.dot(key_source, token_kv, preferred_element_type=jnp.float32).astype(jnp.bfloat16)
    token_width = token_q.shape[0]
    token_head = token_width // TH
    query_rows = queries.reshape(tok_rows, TH, token_head)
    key_rows = keyvals[:, :token_width].reshape(-1, TH, token_head)
    value_rows = keyvals[:, token_width:].reshape(-1, TH, token_head)
    token_scores = jnp.einsum(
        "qhd,khd->hqk", query_rows, key_rows, preferred_element_type=jnp.float32
    ) / math.sqrt(token_head)
    token_scores = token_scores + pair_bias.astype(jnp.float32)
    block_top = jnp.max(token_scores, axis=2)
    block_exp = jnp.exp(token_scores - block_top[:, :, None])
    token_weights = block_exp.astype(jnp.bfloat16)
    block_total = jnp.sum(block_exp, axis=2)
    block_mix = jnp.einsum(
        "hqk,khd->qhd", token_weights, value_rows, preferred_element_type=jnp.float32
    )
    top_rows = block_top.T
    total_rows = block_total.T
    merged = combined_all((top_rows, total_rows, block_mix), "ka", merge_parts)
    token_mix = (
        (merged[2] / merged[1][:, :, None]).reshape(tok_rows, token_width).astype(jnp.bfloat16)
    )
    tokens_out = (
        token_repr.astype(jnp.float32)
        + jnp.dot(token_mix, token_o, preferred_element_type=jnp.float32)
    ).astype(jnp.bfloat16)
    return (atom_out, tokens_out)


def solution(mesh):
    return jax.shard_map(
        body,
        mesh=mesh,
        in_specs=(
            P("pb", None),
            P(),
            P(),
            P(),
            P(None, "pb", None),
            P("pb"),
            P("pb"),
            P(),
            P(),
            P(),
            P(),
            P(),
            P(None, "pb", "ka"),
        ),
        out_specs=(P("pb", None), P("pb", None)),
        check_vma=False,
    )
```

profile of v0, /device:TPU:0, one launch (start us, length us, event | category | flops | bytes accessed | tf_op | source)
XLA Modules:
  0.0 517.4 jit_solution(4085761308660909534)
XLA Ops:
  17.7 2.7 slice.60
  20.4 2.9 reshape.174
  23.3 2.7 pad_maximum_fusion
  26.0 47.8 %gather_fusion = bf16[12288,256]{1,0:T(8,128)(2,1)} fusion(bf16[3200,256]{1,0:T(8,128)(2,1)} %pad_maximum_fusion, s32[12288]{0:T(1024)S(1)} %fusion.51), kind=kCustom, calls=%fused_computation | custom fusion | bytes 12632064 | tf_op jit(solution)/shard_map/jit(_take)/gather | solution.py:94
  73.8 8.7 %copy.44 = bf16[96,128,256]{1,2,0:T(8,128)(2,1)} copy(bf16[96,128,256]{2,1,0:T(8,128)(2,1)} %bitcast.70) | data formatting | bytes 12582912 | tf_op jit(solution)/shard_map/jit(_take)/gather | solution.py:94
  82.4 3.4 broadcast_select_fusion
  85.8 4.0 fusion.63
  89.8 8.4 %fusion.66 = (f32[4,96,32]{2,1,0:T(8,128)S(1)}, f32[4,96,32,128]{3,2,1,0:T(8,128)}) fusion(bf16[4,96,32,128]{3,2,1,0:T(8,128)(2,1)} %bitcast.83, pred[96,128]{1,0:T(8,128)(4,1)S(1)} %get-tuple-element.230, bf16[96,32,4,32]{3,2,1,0:T(4,128)(2,1)} %reshape.174, bf16[96,128,4,32]{1,3,2,0:T(8,128)(2,1)} %bitcast.74), kind=kOutput, calls=%fused_computation.101 | convolution fusion | flops 110100608 | bytes 13430784 | tf_op jit(solution)/shard_map/sub | solution.py:105
  98.3 4.9 convert_bitcast_fusion
  103.2 3.7 copy.49
  106.9 5.6 %convert_element_type.86 = bf16[3072,128]{0,1:T(8,128)(2,1)} reshape(bf16[96,32,4,32]{1,0,3,2:T(8,128)(2,1)} %copy.49) | data formatting | bytes 1572864 | tf_op jit(solution)/shard_map/convert_element_type | solution.py:110
  114.0 2.9 multiply_convert_fusion
  117.3 7.3 %collective-permute-start.2 = (bf16[384,768]{1,0:T(8,128)(2,1)S(1)}, bf16[384,768]{1,0:T(8,128)(2,1)S(1)}, u32[]{:S(2)}, u32[]{:S(2)}) collective-permute-start(bf16[384,768]{1,0:T(8,128)(2,1)S(1)} %convolution_convert_fusion.3), channel_id=1, source_target_pairs={{0,8},{8,16},{16,24},{24,32},{32,40},{40,48},{48,56},{56,64},{64,7... | collective-permute-start | bytes 1769480 | tf_op jit(solution)/shard_map/ppermute | solution.py:35
  124.7 5.1 collective-permute-start.3
  138.1 80.3 %all-gather.6.cloned.1.call-done = bf16[6144,768]{1,0:T(8,128)(2,1)} async-done(((bf16[384,768]{1,0:T(8,128)(2,1)}), bf16[6144,768]{1,0:T(8,128)(2,1)}) %all-gather.6.cloned.1.call-update) | async-done | bytes 9437200 | tf_op jit(solution)/shard_map/all_gather | solution.py:145
  218.4 3.3 convolution_convert_fusion.1
  223.2 11.0 %fusion.67 = (f32[16,384]{1,0:T(8,128)S(1)}, f32[16,384,768]{2,1,0:T(8,128)}) fusion(bf16[16,384,768]{2,1,0:T(8,128)(2,1)} %param.27, bf16[384,16,48]{0,2,1:T(8,128)(2,1)} %bitcast.75, bf16[768,16,48]{0,2,1:T(8,128)(2,1)S(1)} %bitcast.72), kind=kOutput, calls=%fused_computation.102 | convolution fusion | flops 471853056 | bytes 30105600 | tf_op jit(solution)/shard_map/qhd,khd->hqk/dot_general | solution.py:155
  234.1 9.0 %fusion.34 = f32[384,16,48]{0,2,1:T(8,128)} fusion(bf16[768,16,48]{0,2,1:T(8,128)(2,1)S(1)} %bitcast.71, f32[16,384,768]{2,1,0:T(8,128)} %get-tuple-element.235, f32[16,384]{1,0:T(8,128)S(1)} %get-tuple-element.234), kind=kOutput, calls=%fused_computation.57 | convolution fusion | flops 462422016 | bytes 21258240 | tf_op jit(solution)/shard_map/hqk,khd->qhd/dot_general | solution.py:163
  243.1 43.7 %all-gather = f32[3072,16]{0,1:T(8,128)S(1)} all-gather(f32[384,16]{0,1:T(8,128)S(1)} %bitcast.81), channel_id=2, replica_groups=mesh['pb'=16,'ka'=8] {'ka'}, dimensions={0}, use_global_device_ids=true | all-gather | bytes 221184 | tf_op jit(solution)/shard_map/all_gather | solution.py:39
  286.8 8.5 %fusion.6 = f32[16,384]{1,0:T(8,128)S(1)} fusion(f32[16,384,768]{2,1,0:T(8,128)} %get-tuple-element.235, f32[16,384]{1,0:T(8,128)S(1)} %get-tuple-element.234), kind=kLoop, calls=%fused_computation.16 | loop fusion | flops 9431040 | bytes 18923520 | tf_op jit(solution)/shard_map/reduce_sum | solution.py:162
  295.3 33.9 %all-gather.1 = f32[3072,16]{0,1:T(8,128)S(1)} all-gather(f32[384,16]{0,1:T(8,128)S(1)} %bitcast.82), channel_id=3, replica_groups=mesh['pb'=16,'ka'=8] {'ka'}, dimensions={0}, use_global_device_ids=true | all-gather | bytes 221184 | tf_op jit(solution)/shard_map/all_gather | solution.py:39
  329.3 106.4 %all-gather.8.cloned.1.call-done = f32[3072,16,48]{0,2,1:T(8,128)} async-done(((f32[384,16,48]{0,2,1:T(8,128)}), f32[3072,16,48]{0,2,1:T(8,128)}) %all-gather.8.cloned.1.call-update) | async-done | bytes 9437200 | tf_op jit(solution)/shard_map/all_gather | solution.py:39
  439.2 19.5 %copy.60 = f32[3072,16,48]{2,1,0:T(8,128)} copy(f32[3072,16,48]{0,2,1:T(8,128)} %all-gather.8.cloned.1.call-done) | data formatting | bytes 18874368 | tf_op jit(solution)/shard_map/while | solution.py:45
  458.7 45.1 %while.19 = (s32[]{:T(128)}, f32[384,16]{0,1:T(8,128)S(1)}, f32[384,16]{0,1:T(8,128)S(1)}, f32[384,16,48]{2,1,0:T(8,128)}, f32[8,384,16]{1,0,2:T(8,128)S(1)}, /*...) while((s32[]{:T(128)}, f32[384,16]{0,1:T(8,128)S(1)}, ...), condition=%wide.region_11.12_spmd, body=%wide.region_10.11_spmd.sunk | while | flops 921605 | bytes 3981455 | solution.py:45
  459.0 6.1 %fusion.94 = f32[384,16,48]{2,1,0:T(8,128)} fusion(f32[8,384,16,48]{3,2,1,0:T(8,128)} %get-tuple-element.317, s32[]{:T(128)S(6)} %select_n.66, f32[384,16,48]{2,1,0:T(8,128)} %get-tuple-element.304, f32[384,16]{1,0:T(8,128)S(1)} %copy.97, f32[384,16]{1,0:T(8,128)S(1)} %copy.98), kind=kLoop, calls=%fused_computation.2.clone.1 | loop fusion | flops 884736 | bytes 3588100 | tf_op jit(solution)/shard_map/while/body/eval_jaxpr/add | solution.py:64
  465.5 6.1 %fusion.94 = f32[384,16,48]{2,1,0:T(8,128)} fusion(f32[8,384,16,48]{3,2,1,0:T(8,128)} %get-tuple-element.317, s32[]{:T(128)S(6)} %select_n.66, f32[384,16,48]{2,1,0:T(8,128)} %get-tuple-element.304, f32[384,16]{1,0:T(8,128)S(1)} %copy.97, f32[384,16]{1,0:T(8,128)S(1)} %copy.98), kind=kLoop, calls=%fused_computation.2.clone.1 | loop fusion | flops 884736 | bytes 3588100 | tf_op jit(solution)/shard_map/while/body/eval_jaxpr/add | solution.py:64
  471.9 6.1 %fusion.94 = f32[384,16,48]{2,1,0:T(8,128)} fusion(f32[8,384,16,48]{3,2,1,0:T(8,128)} %get-tuple-element.317, s32[]{:T(128)S(6)} %select_n.66, f32[384,16,48]{2,1,0:T(8,128)} %get-tuple-element.304, f32[384,16]{1,0:T(8,128)S(1)} %copy.97, f32[384,16]{1,0:T(8,128)S(1)} %copy.98), kind=kLoop, calls=%fused_computation.2.clone.1 | loop fusion | flops 884736 | bytes 3588100 | tf_op jit(solution)/shard_map/while/body/eval_jaxpr/add | solution.py:64
  478.3 6.1 %fusion.94 = f32[384,16,48]{2,1,0:T(8,128)} fusion(f32[8,384,16,48]{3,2,1,0:T(8,128)} %get-tuple-element.317, s32[]{:T(128)S(6)} %select_n.66, f32[384,16,48]{2,1,0:T(8,128)} %get-tuple-element.304, f32[384,16]{1,0:T(8,128)S(1)} %copy.97, f32[384,16]{1,0:T(8,128)S(1)} %copy.98), kind=kLoop, calls=%fused_computation.2.clone.1 | loop fusion | flops 884736 | bytes 3588100 | tf_op jit(solution)/shard_map/while/body/eval_jaxpr/add | solution.py:64
  484.8 6.1 %fusion.94 = f32[384,16,48]{2,1,0:T(8,128)} fusion(f32[8,384,16,48]{3,2,1,0:T(8,128)} %get-tuple-element.317, s32[]{:T(128)S(6)} %select_n.66, f32[384,16,48]{2,1,0:T(8,128)} %get-tuple-element.304, f32[384,16]{1,0:T(8,128)S(1)} %copy.97, f32[384,16]{1,0:T(8,128)S(1)} %copy.98), kind=kLoop, calls=%fused_computation.2.clone.1 | loop fusion | flops 884736 | bytes 3588100 | tf_op jit(solution)/shard_map/while/body/eval_jaxpr/add | solution.py:64
  491.2 6.1 %fusion.94 = f32[384,16,48]{2,1,0:T(8,128)} fusion(f32[8,384,16,48]{3,2,1,0:T(8,128)} %get-tuple-element.317, s32[]{:T(128)S(6)} %select_n.66, f32[384,16,48]{2,1,0:T(8,128)} %get-tuple-element.304, f32[384,16]{1,0:T(8,128)S(1)} %copy.97, f32[384,16]{1,0:T(8,128)S(1)} %copy.98), kind=kLoop, calls=%fused_computation.2.clone.1 | loop fusion | flops 884736 | bytes 3588100 | tf_op jit(solution)/shard_map/while/body/eval_jaxpr/add | solution.py:64
  497.6 6.1 %fusion.94 = f32[384,16,48]{2,1,0:T(8,128)} fusion(f32[8,384,16,48]{3,2,1,0:T(8,128)} %get-tuple-element.317, s32[]{:T(128)S(6)} %select_n.66, f32[384,16,48]{2,1,0:T(8,128)} %get-tuple-element.304, f32[384,16]{1,0:T(8,128)S(1)} %copy.97, f32[384,16]{1,0:T(8,128)S(1)} %copy.98), kind=kLoop, calls=%fused_computation.2.clone.1 | loop fusion | flops 884736 | bytes 3588100 | tf_op jit(solution)/shard_map/while/body/eval_jaxpr/add | solution.py:64
  507.7 2.9 fusion.37
  (99 shorter events, 32.1 us)
Async XLA Ops:
  7.2 211.3 %copy-start = (bf16[768,1536]{1,0:T(8,128)(2,1)S(1)}, bf16[768,1536]{1,0:T(8,128)(2,1)}, u32[]{:S(2)}) copy-start(bf16[768,1536]{1,0:T(8,128)(2,1)} %param.25) | copy-start | bytes 7077892
  7.2 10.3 %copy-start.11 = (s32[96]{0:T(128)S(1)}, s32[96]{0:T(128)}, u32[]{:S(2)}) copy-start(s32[96]{0:T(128)} %param.20) | copy-start | bytes 1156
  7.2 10.5 %copy-start.8 = (s32[3072]{0:T(1024)S(1)}, s32[3072]{0:T(1024)}, u32[]{:S(2)}) copy-start(s32[3072]{0:T(1024)} %param.21) | copy-start | bytes 36868
  7.2 211.2 %all-gather.6.cloned.1.call-start = ((), (), s32[]{:S(2)}) async-start(), calls=%async_computation | async-start | bytes 10027008 | tf_op jit(solution)/shard_map/all_gather | solution.py:145
  13.1 1.4 copy-start.3
  14.6 5.8 %slice-start.1 = ((bf16[3072,384]{1,0:T(8,128)(2,1)}), bf16[3072,128]{1,0:T(8,128)(2,1)S(1)}, s32[]{:S(2)}) async-start(bf16[3072,384]{1,0:T(8,128)(2,1)} %copy-done.3), calls=%async_computation.3 | async-start | bytes 1572864 | tf_op jit(solution)/shard_map/slice | solution.py:97
  14.6 8.7 %collective-permute-start = (bf16[64,256]{1,0:T(8,128)(2,1)S(1)}, bf16[64,256]{1,0:T(8,128)(2,1)S(1)}, u32[]{:S(2)}, u32[]{:S(2)}) collective-permute-start(bf16[64,256]{1,0:T(8,128)(2,1)S(1)} %get-tuple-element.228), channel_id=1, source_target_pairs={{0,8},{8,16},{16,24},{24,32},{32,40},{40,48},{48,56},{56,64},{64,7... | collective-permute-start | bytes 98312 | tf_op jit(solution)/shard_map/ppermute | solution.py:23
  16.0 7.3 %collective-permute-start.1 = (bf16[64,256]{1,0:T(8,128)(2,1)S(1)}, bf16[64,256]{1,0:T(8,128)(2,1)S(1)}, u32[]{:S(2)}, u32[]{:S(2)}) collective-permute-start(bf16[64,256]{1,0:T(8,128)(2,1)S(1)} %get-tuple-element.229), channel_id=1, source_target_pairs={{8,0},{16,8},{24,16},{32,24},{40,32},{48,40},{56,48},{64,56},{72,6... | collective-permute-start | bytes 98312 | tf_op jit(solution)/shard_map/ppermute | solution.py:25
  106.8 5.6 %copy-start.2 = (bf16[3072,128]{1,0:T(8,128)(2,1)S(1)}, bf16[3072,128]{1,0:T(8,128)(2,1)}, u32[]{:S(2)}) copy-start(bf16[3072,128]{1,0:T(8,128)(2,1)} %param.15) | copy-start | bytes 2359300
  106.8 5.6 %copy-start.7 = (bf16[128,128]{1,0:T(8,128)(2,1)S(1)}, bf16[128,128]{1,0:T(8,128)(2,1)}, u32[]{:S(2)}) copy-start(bf16[128,128]{1,0:T(8,128)(2,1)} %param.18) | copy-start | bytes 98308
  106.9 7.1 %copy-start.10 = (bf16[128,768]{1,0:T(8,128)(2,1)S(1)}, bf16[128,768]{1,0:T(8,128)(2,1)}, u32[]{:S(2)}) copy-start(bf16[128,768]{1,0:T(8,128)(2,1)} %param.22) | copy-start | bytes 589828
  114.0 2.9 copy-start.6
  117.3 13.3 %collective-permute-start.2 = (bf16[384,768]{1,0:T(8,128)(2,1)S(1)}, bf16[384,768]{1,0:T(8,128)(2,1)S(1)}, u32[]{:S(2)}, u32[]{:S(2)}) collective-permute-start(bf16[384,768]{1,0:T(8,128)(2,1)S(1)} %convolution_convert_fusion.3), channel_id=1, source_target_pairs={{0,8},{8,16},{16,24},{24,32},{32,40},{40,48},{48,56},{56,64},{64,7... | collective-permute-start | bytes 1769480 | tf_op jit(solution)/shard_map/ppermute | solution.py:35
  124.7 5.9 %collective-permute-start.3 = (bf16[384]{0:T(512)(128)(2,1)S(1)}, bf16[384]{0:T(512)(128)(2,1)S(1)}, u32[]{:S(2)}, u32[]{:S(2)}) collective-permute-start(bf16[384]{0:T(512)(128)(2,1)S(1)} %fusion.48), channel_id=1, source_target_pairs={{0,8},{8,16},{16,24},{24,32},{32,40},{40,48},{48,56},{56,64},{64,7... | collective-permute-start | bytes 2312 | tf_op jit(solution)/shard_map/ppermute | solution.py:35
  130.6 3.2 copy-start.9
  133.0 0.8 copy-start.4
  134.9 300.8 %all-gather.8.cloned.1.call-start = ((), (), s32[]{:S(2)}) async-start(), calls=%async_computation.1 | async-start | bytes 10616832 | tf_op jit(solution)/shard_map/all_gather | solution.py:39
  435.7 1.3 slice-start
  503.7 0.6 copy-start.5
  504.3 6.2 %copy-start.1 = (bf16[768,1536]{1,0:T(8,128)(2,1)S(1)}, bf16[768,1536]{1,0:T(8,128)(2,1)}, u32[]{:S(2)}) copy-start(bf16[768,1536]{1,0:T(8,128)(2,1)} %param.25) | copy-start | bytes 7077892
Sparse Core Ops, SparseCore 0:
  135.0 83.3 all-gather.5
  243.3 192.3 all-gather.7
where the time goes:
time: 522 us; the launch traced here: 517 us
  waiting for transfers between devices  187 us (36%)
  local copies, waits for them, and re-layouts  108 us (21%)
  blocking collectives  77.5 us (15%)
  other arithmetic  64.2 us (12%)
  matrix products  50.9 us (10%)
  starting transfers between devices  15.3 us (3%)
  between operations  14.4 us (3%)
    all_gather x1, waiting for transfers between devices, combined_all(): everything = jax.tree.map(lambda part: lax.all_gather(part, axis), shard)  106 us
    all_gather x1, waiting for transfers between devices, body(): every_row = lax.all_gather(token_normed, 'pb', axis=0, tiled=True)  80.3 us
    all_gather x2, blocking collectives, combined_all(): everything = jax.tree.map(lambda part: lax.all_gather(part, axis), shard)  77.5 us
    gather x2, local copies, waits for them, and re-layouts, body(): gathered = jnp.take(padded, key_index + half_win, axis=0)  56.4 us
    add x7, other arithmetic, merge_parts(): mixed_one * scale_one[:, :, None] + mixed_two * scale_two[:, :, None]  42.7 us
    while x3, local copies, waits for them, and re-layouts, combined_all(): return lax.fori_loop(1, lax.axis_size(axis), hop, leading)  24.3 us
    ppermute x2, starting transfers between devices, from_behind(): return lax.ppermute(shard, axis, pairs)  12.4 us
    dot_general x1, matrix products, body(): jnp.einsum('qhd,khd->hqk', query_rows, key_rows, preferred_element_type=j...  11 us
  transfers between devices with their start and end apart: 6, of which 3 were waited for; matrix products, arithmetic and copies ran while one was open for 4% of the time, Pallas kernels for 0%

commit v1 on v0

v1 whole, which is shorter than its diff:
```python
import functools
import math

import jax
import jax.numpy as jnp
from jax import lax
from jax.experimental import pallas as pl
from jax.experimental.pallas import tpu as pltpu
from jax.sharding import PartitionSpec as P

F32, BF16, I32 = jnp.float32, jnp.bfloat16, jnp.int32
AR, HALO, TAIL, WQ, WK = 3072, 64, 384, 32, 128
EXT = AR + 2 * HALO
TR, CT, TH, HD = 384, 768, 16, 48
PIECE = TR // 8
WINDOWS = AR // WQ
UNROLL = 4
CHUNKS = ((0, 6, 0), (6, 11, 256), (11, 16, 512))
NT = (((1,), (1,)), ((), ()))
NN = (((1,), (0,)), ((), ()))


def iota(shape, dim):
    return lax.broadcasted_iota(I32, shape, dim)


def mm(a, b, dims=NN):
    return lax.dot_general(a, b, dims, preferred_element_type=F32)


def normed(x, gain):
    centre = jnp.mean(x, axis=-1, keepdims=True)
    diff = x - centre
    spread = jnp.mean(diff * diff, axis=-1, keepdims=True)
    return (diff * lax.rsqrt(spread + 1e-05) * gain).astype(BF16)


def kernel(
    shift_ref,
    atoms_h,
    again_h,
    qkv_h,
    proj_h,
    abias_h,
    ids_h,
    agg_h,
    tgain_h,
    wq_h,
    wkv_h,
    wo_h,
    pair_h,
    aout_h,
    tout_h,
    xs,
    again,
    wqkv,
    wproj,
    ab,
    ids,
    wagg,
    tgain,
    wq,
    wkv,
    wo,
    pbm,
    qs,
    kf,
    vf,
    ms,
    ao,
    acc,
    rep,
    nrm,
    qt,
    kt,
    kk,
    vv,
    osc,
    mlb,
    mixb,
    rbuf,
    rml,
    obuf,
    lsem,
    psem,
    osem,
    hs,
    hr,
    xsem,
    xrsem,
    fs,
    fr,
    rs,
    rr,
    gs,
    gr,
):
    p = lax.axis_index("pb")
    k = lax.axis_index("ka")
    c = lax.rem(p, 2)
    cp = lax.div(p, 2)
    last = 15
    barrier = pltpu.get_barrier_semaphore()

    def dev(pb, ka):
        return {"pb": pb, "ka": ka}

    def hello(pb, ka):
        pl.semaphore_signal(barrier, inc=1, device_id=dev(pb, ka), device_id_type=pl.DeviceIdType.MESH)

    def send(src, dst, ssem, rsem, pb, ka):
        return pltpu.make_async_remote_copy(
            src_ref=src,
            dst_ref=dst,
            send_sem=ssem,
            recv_sem=rsem,
            device_id=dev(pb, ka),
            device_id_type=pl.DeviceIdType.MESH,
        )

    @pl.when(p > 0)
    def _():
        hello(p - 1, k)

    @pl.when(p < last)
    def _():
        hello(p + 1, k)

    for i in range(1, 8):
        hello(lax.rem(cp + i, 8) * 2 + c, cp)
        hello(p, lax.rem(k + i, 8))

    @pl.when(k != cp)
    def _():
        for s in range(8):
            hello(2 * k + c, s)

    copies = {}

    def load(name, src, dst, sem):
        copies[name] = pltpu.make_async_copy(src, dst, sem)
        copies[name].start()

    load("atoms", atoms_h, xs.at[pl.ds(HALO, AR)], lsem.at[0])
    load("again", again_h, again, lsem.at[1])
    load("qkv", qkv_h, wqkv, lsem.at[2])
    load("abias", abias_h, ab, lsem.at[3])
    load("proj", proj_h, wproj, lsem.at[4])
    load("agg", agg_h, wagg, lsem.at[5])
    load("ids", ids_h, ids.at[:, pl.ds(0, AR)], lsem.at[6])
    load("tgain", tgain_h, tgain, lsem.at[7])
    load("wq", wq_h, wq, lsem.at[8])
    load("wkv", wkv_h, wkv, lsem.at[9])
    load("wo", wo_h, wo, lsem.at[10])
    load("pair", pair_h, pbm, psem)

    def project(row, rows, queries):
        x = xs[pl.ds(row, rows), :].astype(F32)
        n = normed(x, again[...])
        y = mm(n, wqkv[...])
        if queries:
            qs[pl.ds(row - HALO, rows), :] = y[:, 0:128].astype(BF16)
        kf[pl.ds(row, rows), :] = y[:, 128:256].astype(BF16).astype(F32)
        vf[pl.ds(row, rows), :] = y[:, 256:384].astype(BF16).astype(F32)

    copies["atoms"].wait()
    copies["again"].wait()
    copies["qkv"].wait()

    def project_own(i, carry):
        project(pl.multiple_of(HALO + i * 384, 64), 384, True)
        return carry

    lax.fori_loop(0, AR // 384, project_own, 0)

    greeted = 14 + jnp.where(p > 0, 1, 0) + jnp.where(p < last, 1, 0) + jnp.where(k != cp, 8, 0)
    pl.semaphore_wait(barrier, greeted)

    right = jnp.minimum(p + 1, last)
    left = jnp.maximum(p - 1, 0)
    to_right = send(
        atoms_h.at[pl.ds(AR - HALO, HALO)], xs.at[pl.ds(0, HALO)], hs.at[0], hr.at[0], right, k
    )
    to_left = send(
        atoms_h.at[pl.ds(0, HALO)], xs.at[pl.ds(HALO + AR, HALO)], hs.at[1], hr.at[1], left, k
    )
    ids_right = send(
        ids_h.at[:, pl.ds(AR - TAIL, TAIL)], ids.at[:, pl.ds(AR, TAIL)], hs.at[2], hr.at[2], right, k
    )
    tail_right = send(
        ao.at[pl.ds(AR - TAIL, TAIL)], ao.at[pl.ds(AR, TAIL)], hs.at[3], hr.at[3], right, k
    )

    @pl.when(p < last)
    def _():
        to_right.start()
        ids_right.start()

    @pl.when(p > 0)
    def _():
        to_left.start()

    copies["abias"].wait()
    copies["proj"].wait()

    head_mask = jnp.where(
        (iota((128, 128), 0) >> 5) == (iota((128, 128), 1) >> 5), 1.0, 0.0
    ).astype(BF16)
    lane_head = iota((WQ, 128), 1) >> 5
    ones = jnp.ones((WK, 128), BF16)
    scale = 1.0 / math.sqrt(32.0)

    def by_head(o):
        return jnp.where(
            lane_head == 0,
            o[0:32],
            jnp.where(lane_head == 1, o[32:64], jnp.where(lane_head == 2, o[64:96], o[96:128])),
        )

    def window(b, masked):
        base = pl.multiple_of(b * WQ, WQ)
        first = base + jnp.clip(shift_ref[b], -HALO, WQ - HALO)
        kw = kf[pl.ds(first + HALO, WK), :].astype(BF16)
        vw = vf[pl.ds(first + HALO, WK), :].astype(BF16)
        q = qs[pl.ds(base, WQ), :]
        q4 = jnp.concatenate([q, q, q, q], axis=0) * head_mask
        s = mm(q4, kw, NT) * scale
        bias = ab[:, pl.ds(base, WQ), :].reshape(128, WK).astype(F32)
        s = s + bias
        if masked:
            j = first + p * AR + iota((1, WK), 1)
            s = jnp.where((j >= 0) & (j < AR * 16), s, -1e30)
        top = jnp.max(s, axis=-1, keepdims=True)
        w = jnp.exp(s - top).astype(BF16)
        o = mm(w, jnp.concatenate([vw, ones], axis=1))
        ms[pl.ds(base, WQ), :] = (by_head(o[:, 0:128]) / by_head(o[:, 128:256])).astype(BF16)

    def windows(lo, hi, masked):
        def group(g, carry):
            for u in range(UNROLL):
                window(g * UNROLL + u, masked)
            return carry

        lax.fori_loop(lo // UNROLL, hi // UNROLL, group, 0)

    def finish_rows(row, rows):
        r = pl.ds(row, rows)
        y = xs[pl.ds(row + HALO, rows), :].astype(F32) + mm(ms[r, :], wproj[...])
        ao[r, :] = y.astype(BF16)

    windows(24, 84, False)

    @pl.when(p > 0)
    def _():
        to_right.wait_recv()

    @pl.when(p < last)
    def _():
        to_left.wait_recv()

    @pl.when(p == 0)
    def _():
        xs[pl.ds(0, HALO), :] = jnp.zeros((HALO, 128), BF16)

    @pl.when(p == last)
    def _():
        xs[pl.ds(HALO + AR, HALO), :] = jnp.zeros((HALO, 128), BF16)

    project(0, HALO, False)
    project(HALO + AR, HALO, False)
    windows(84, 96, True)
    finish_rows(AR - TAIL, TAIL)

    @pl.when(p < last)
    def _():
        tail_right.start()

    windows(0, 24, True)

    def finish(i, carry):
        finish_rows(pl.multiple_of(i * 384, 384), 384)
        return carry

    lax.fori_loop(0, (AR - TAIL) // 384, finish, 0)
    aout_copy = pltpu.make_async_copy(ao.at[pl.ds(0, AR)], aout_h, osem.at[0])
    aout_copy.start()

    copies["agg"].wait()
    copies["ids"].wait()
    copies["tgain"].wait()
    first_token = p * TR

    def pool(row, rows):
        v = mm(ao[pl.ds(row, rows), :], wagg[...])
        hidden = (0.5 * v * (1.0 + jnp.tanh(0.5 * v))).astype(BF16)
        local = ids[:, pl.ds(row, rows)] - first_token
        hot = jnp.where(local == iota((TR, rows), 0), 1.0, 0.0)
        acc[...] += mm(hot.astype(BF16), hidden)
        osc[:, 0:128] += jnp.broadcast_to(jnp.sum(hot, axis=1, keepdims=True), (TR, 128))

    acc[...] = jnp.zeros((TR, CT), F32)
    osc[:, 0:128] = jnp.zeros((TR, 128), F32)

    def pool_own(i, carry):
        pool(pl.multiple_of(i * 768, 128), 768)
        return carry

    lax.fori_loop(0, AR // 768, pool_own, 0)

    @pl.when(p > 0)
    def _():
        ids_right.wait_recv()
        tail_right.wait_recv()

    @pl.when(p == 0)
    def _():
        ids[:, pl.ds(AR, TAIL)] = jnp.full((1, TAIL), -1, I32)
        ao[pl.ds(AR, TAIL), :] = jnp.zeros((TAIL, 128), BF16)

    pool(AR, TAIL)
    repr_f = (acc[...] / osc[:, 0:1]).astype(BF16)
    rep[...] = repr_f
    nrm[...] = normed(repr_f.astype(F32), tgain[...])

    def rows48(i):
        return pl.ds(pl.multiple_of(i * PIECE, 16), PIECE)

    def half(i):
        return pl.ds(pl.multiple_of(i * TR, 16), TR)

    outs = []
    for i in range(1, 8):
        target = lax.rem(cp + i, 8) * 2 + c
        outs.append(
            send(
                nrm.at[rows48(k)],
                kt.at[pl.ds(pl.multiple_of(c * TR + k * PIECE, 16), PIECE)],
                xsem.at[i],
                xrsem.at[k],
                target,
                cp,
            )
        )
        outs[-1].start()

    copies["wq"].wait()
    qt[...] = mm(nrm[...], wq[...]).astype(BF16)

    @pl.when(k == cp)
    def _():
        kt[half(c), :] = nrm[...]

    @pl.when(k != cp)
    def _():
        for s in range(8):
            send(
                nrm.at[rows48(0)],
                kt.at[pl.ds(pl.multiple_of(c * TR + s * PIECE, 16), PIECE)],
                xsem.at[0],
                xrsem.at[s],
                p,
                k,
            ).wait_recv()

    partner = p + 1 - 2 * c
    fwd = send(kt.at[half(c)], kt.at[half(c)], fs, fr, partner, k)
    fwd.start()
    copies["wkv"].wait()
    back = send(kt.at[half(c)], kt.at[half(1 - c)], fs, fr, partner, k)
    back.wait_recv()

    def keyvals(j, carry):
        cols = pl.ds(pl.multiple_of(j * 256, 256), 256)
        kk[:, cols] = mm(kt[...], wkv[:, cols]).astype(BF16)
        vcols = pl.ds(pl.multiple_of(j * 256 + CT, 256), 256)
        vv[:, cols] = mm(kt[...], wkv[:, vcols]).astype(BF16)
        return carry

    lax.fori_loop(0, CT // 256, keyvals, 0)
    copies["pair"].wait()
    tscale = 1.0 / math.sqrt(float(HD))
    rb = 128

    def head(h, carry):
        tile = jnp.minimum(lax.div(h * HD, 128), 4)
        lane0 = pl.multiple_of(tile * 128, 128)
        off = h * HD - lane0
        lanes = pl.ds(lane0, 256)
        keys = kk[:, lanes]
        values = vv[:, lanes]
        lane = iota((rb, 256), 1)
        mask = (lane >= off) & (lane < off + HD)
        l128 = iota((rb, 128), 1)
        for r in range(TR // rb):
            rows = pl.ds(r * rb, rb)
            q = jnp.where(mask, qt[rows, lanes].astype(F32), 0.0).astype(BF16)
            s = mm(q, keys, NT) * tscale + pbm[h, rows, :].astype(F32)
            top = jnp.max(s, axis=-1, keepdims=True)
            e = jnp.exp(s - top)
            total = jnp.sum(e, axis=-1, keepdims=True)
            o = mm(e.astype(BF16), values)
            osc[rows, lanes] = jnp.where(mask, o, osc[rows, lanes])
            mlb[rows, :] = jnp.where(
                l128 == h, top, jnp.where(l128 == h + TH, total, mlb[rows, :])
            )
        return carry

    sends = []
    for n, (lo, hi, col) in enumerate(CHUNKS):
        lax.fori_loop(lo, hi, head, 0)
        cols = pl.ds(col, 256)
        mixb[:, cols] = osc[:, cols].astype(BF16)
        for i in range(1, 8):
            peer = lax.rem(k + i, 8)
            sends.append(
                send(
                    mixb.at[rows48(peer), cols],
                    rbuf.at[i, :, cols],
                    rs.at[n, i],
                    rr.at[n, i],
                    p,
                    peer,
                )
            )
            sends[-1].start()
    for i in range(1, 8):
        peer = lax.rem(k + i, 8)
        sends.append(send(mlb.at[rows48(peer)], rml.at[i], rs.at[3, i], rr.at[3, i], p, peer))
        sends[-1].start()

    rbuf[0, :, :] = mixb[rows48(k), :]
    rml[0, :, :] = mlb[rows48(k), :]
    copies["wo"].wait()
    for copy in sends:
        copy.wait_recv()

    ml = rml[...]
    tot = pltpu.roll(ml.reshape(8 * PIECE, 128), 128 - TH, 1).reshape(8, PIECE, 128)
    real = iota((8, PIECE, 128), 2) < TH
    ml = jnp.where(real, ml, 0.0)
    tot = jnp.where(real, tot, 1.0)
    top = jnp.max(ml, axis=0, keepdims=True)
    factor = jnp.exp(ml - top)
    weight = factor / jnp.sum(factor * tot, axis=0, keepdims=True)
    weight = weight.reshape(8 * PIECE, 128)
    high = weight.astype(BF16)
    low = (weight - high.astype(F32)).astype(BF16)
    i0, j0 = iota((128, CT), 0) * HD, iota((128, CT), 1)
    expand = jnp.where((j0 >= i0) & (j0 < i0 + HD), 1.0, 0.0).astype(BF16)
    wide = (mm(high, expand) + mm(low, expand)).reshape(8, PIECE, CT)
    mix = jnp.sum(wide * rbuf[...].astype(F32), axis=0).astype(BF16)
    obuf[...] = (rep[rows48(k), :].astype(F32) + mm(mix, wo[...])).astype(BF16)
    own = pltpu.make_async_copy(obuf, tout_h.at[rows48(k)], osem.at[1])
    own.start()
    gathers = []
    for i in range(1, 8):
        peer = lax.rem(k + i, 8)
        gathers.append(send(obuf, tout_h.at[rows48(k)], gs.at[i], gr.at[i], p, peer))
        gathers[-1].start()
    own.wait()
    aout_copy.wait()
    for i in range(1, 8):
        src = lax.rem(k + 8 - i, 8)
        send(obuf, tout_h.at[rows48(src)], gs.at[i], gr.at[i], p, src).wait_recv()
    for copy in gathers + sends + outs:
        copy.wait_send()
    fwd.wait_send()

    @pl.when(p < last)
    def _():
        to_right.wait_send()
        ids_right.wait_send()
        tail_right.wait_send()

    @pl.when(p > 0)
    def _():
        to_left.wait_send()


def body(
    atoms,
    atom_gain,
    atom_qkv,
    atom_proj,
    atom_bias,
    window_shift,
    token_of_atom,
    agg_weight,
    token_gain,
    token_q,
    token_kv,
    token_o,
    pair_bias,
):
    hbm = pl.BlockSpec(memory_space=pl.ANY)
    vm = pltpu.VMEM
    dma = pltpu.SemaphoreType.DMA
    return pl.pallas_call(
        kernel,
        out_shape=(
            jax.ShapeDtypeStruct((AR, 128), BF16),
            jax.ShapeDtypeStruct((TR, CT), BF16),
        ),
        in_specs=[pl.BlockSpec(memory_space=pltpu.SMEM)] + [hbm] * 12,
        out_specs=(hbm, hbm),
        scratch_shapes=[
            vm((EXT, 128), BF16),
            vm((1, 128), F32),
            vm((128, 384), BF16),
            vm((128, 128), BF16),
            vm((4, AR, WK), BF16),
            vm((1, AR + TAIL), I32),
            vm((128, CT), BF16),
            vm((1, CT), F32),
            vm((CT, CT), BF16),
            vm((CT, 2 * CT), BF16),
            vm((CT, CT), BF16),
            vm((TH, TR, 2 * TR), BF16),
            vm((AR, 128), BF16),
            vm((EXT, 128), F32),
            vm((EXT, 128), F32),
            vm((AR, 128), BF16),
            vm((AR + TAIL, 128), BF16),
            vm((TR, CT), F32),
            vm((TR, CT), BF16),
            vm((TR, CT), BF16),
            vm((TR, CT), BF16),
            vm((2 * TR, CT), BF16),
            vm((2 * TR, CT), BF16),
            vm((2 * TR, CT), BF16),
            vm((TR, CT), F32),
            vm((TR, 128), F32),
            vm((TR, CT), BF16),
            vm((8, PIECE, CT), BF16),
            vm((8, PIECE, 128), F32),
            vm((PIECE, CT), BF16),
            dma((11,)),
            dma,
            dma((2,)),
            dma((4,)),
            dma((4,)),
            dma((8,)),
            dma((8,)),
            dma,
            dma,
            dma((4, 8)),
            dma((4, 8)),
            dma((8,)),
            dma((8,)),
        ],
        compiler_params=pltpu.CompilerParams(
            collective_id=0, has_side_effects=True, vmem_limit_bytes=60 * 1024 * 1024
        ),
    )(
        window_shift,
        atoms,
        atom_gain.reshape(1, 128),
        atom_qkv,
        atom_proj,
        atom_bias,
        token_of_atom.reshape(1, AR),
        agg_weight,
        token_gain.reshape(1, CT),
        token_q,
        token_kv,
        token_o,
        pair_bias,
    )


def solution(mesh):
    return jax.shard_map(
        body,
        mesh=mesh,
        in_specs=(
            P("pb", None),
            P(),
            P(),
            P(),
            P(None, "pb", None),
            P("pb"),
            P("pb"),
            P(),
            P(),
            P(),
            P(),
            P(),
            P(None, "pb", "ka"),
        ),
        out_specs=(P("pb", None), P("pb", None)),
        check_vma=False,
    )
```

time: 522 us -> 110 us (0.21)
  waiting for transfers between devices: 187 us -> 0 us
  local copies, waits for them, and re-layouts: 108 us -> 5.25 us
  Pallas kernels: 0 us -> 102 us
  blocking collectives: 77.5 us -> 0 us
  other arithmetic: 64.2 us -> 0 us
  matrix products: 50.9 us -> 0 us
  starting transfers between devices: 15.3 us -> 0 us
  between operations: 14.4 us -> 0.64 us
    all_gather x2 -> x0, waiting for transfers between devices: 187 us -> none  [the longest x1 106 us: combined_all(): everything = jax.tree.map(lambda part: lax.all_gather(part, axis), shard)]
    pallas_call x0 -> x1, Pallas kernels: none -> 102 us  [body(): pl.pallas_call(kernel, out_shape=(jax.ShapeDtypeStruct((AR, 128), BF16),...]
    all_gather x2 -> x0, blocking collectives: 77.5 us -> none  [combined_all(): everything = jax.tree.map(lambda part: lax.all_gather(part, axis), shard)]
    gather x2 -> x0, local copies, waits for them, and re-layouts: 56.4 us -> none  [body(): gathered = jnp.take(padded, key_index + half_win, axis=0)]
    add x16 -> x0, other arithmetic: 42.9 us -> none  [the longest x7 42.7 us: merge_parts(): mixed_one * scale_one[:, :, None] + mixed_two * scale_two[:, :, None]]
    dot_general x11 -> x0, matrix products: 42.5 us -> none  [the longest x1 11 us: body(): jnp.einsum('qhd,khd->hqk', query_rows, key_rows, preferred_element_type=j...]
    while x3 -> x0, local copies, waits for them, and re-layouts: 24.3 us -> none  [combined_all(): return lax.fori_loop(1, lax.axis_size(axis), hop, leading)]
    ppermute x4 -> x0, starting transfers between devices: 15.2 us -> none  [the longest x2 12.4 us: from_behind(): return lax.ppermute(shard, axis, pairs)]
  transfers between devices with their start and end apart: 6 -> 0, of which waited for: 3 -> 0; matrix products, arithmetic and copies ran while one was open for 4% -> 0% of each run, Pallas kernels for 0% -> 0%
where the time goes in v1:
time: 110 us; the launch traced here: 108 us
  Pallas kernels  102 us (93%)
  local copies, waits for them, and re-layouts  5.25 us (5%)
    pallas_call x1, Pallas kernels, body(): pl.pallas_call(kernel, out_shape=(jax.ShapeDtypeStruct((AR, 128), BF16),...  102 us
    unnamed x2, local copies, waits for them, and re-layouts  3.98 us

profile of v1, /device:TPU:0, one launch (start us, length us, event | category | flops | bytes accessed | tf_op | source)
XLA Modules:
  0.0 108.2 jit_solution(9575574775476691819)
XLA Ops:
  0.6 1.3 %reshape.15.tgain_h = f32[1,768]{1,0:T(1,128)} reshape(f32[768]{0:T(1024)} %param.21) | data formatting | bytes 6144 | tf_op jit(solution)/shard_map/reshape | solution.py:563
  1.9 102.3 %shard_map.140 = (bf16[3072,128]{1,0:T(8,128)(2,1)}, bf16[384,768]{1,0:T(8,128)(2,1)}) custom-call(s32[96]{0:T(128)} %shift_ref.1, bf16[3072,128]{1,0:T(8,128)(2,1)} %atoms_h.1, f32[1,128]{1,0:T(1,128)} %bitcast.3, bf16[128,384]{1,0:T(8,128)(2,1)} %qkv_h.1, bf16[128,128]{1,0:T(8,128)(2,1)} %proj_h.1, bf16[4,3072,128]{2,1,0:T(8,128)(2,1)} %abias_h.1, ...), custom_call_target="tpu_custom_call" | custom-call | tf_op jit(solution)/shard_map/pallas_call | solution.py:498
  104.2 2.1 %copy.17 = bf16[3072,128]{1,0:T(8,128)(2,1)} copy(bf16[3072,128]{1,0:T(8,128)(2,1)} %get-tuple-element.4) | data formatting | bytes 1572864
  106.3 1.9 %copy.18 = bf16[384,768]{1,0:T(8,128)(2,1)} copy(bf16[384,768]{1,0:T(8,128)(2,1)} %get-tuple-element.5) | data formatting | bytes 1179648

commit v2 on v1

--- a/solution.py
+++ b/solution.py
@@ -14,8 +14,9 @@
 TR, CT, TH, HD = 384, 768, 16, 48
 PIECE = TR // 8
 WINDOWS = AR // WQ
-UNROLL = 4
-CHUNKS = ((0, 6, 0), (6, 11, 256), (11, 16, 512))
+UNROLL = 8
+CHUNKS = ((0, 6, 0), (6, 12, 256), (12, 16, 512))
+FEATURES = (0, 256, 512)
 NT = (((1,), (1,)), ((), ()))
 NN = (((1,), (0,)), ((), ()))
 
@@ -68,7 +69,10 @@
     vf,
     ms,
     ao,
-    acc,
+    hot,
+    hid,
+    rly,
+    kn,
     rep,
     nrm,
     qt,
@@ -88,6 +92,9 @@
     hr,
     xsem,
     xrsem,
+    rls,
+    rlr,
+    rfs,
     fs,
     fr,
     rs,
@@ -99,6 +106,9 @@
     k = lax.axis_index("ka")
     c = lax.rem(p, 2)
     cp = lax.div(p, 2)
+    zh, zl = lax.rem(cp, 2), lax.rem(k, 2)
+    outer = zh == zl
+    cp_flip, k_flip, p_flip = cp + 1 - 2 * zh, k + 1 - 2 * zl, p + 2 - 4 * zh
     last = 15
     barrier = pltpu.get_barrier_semaphore()
 
@@ -127,10 +137,31 @@
         hello(p + 1, k)
 
     for i in range(1, 8):
-        hello(lax.rem(cp + i, 8) * 2 + c, cp)
         hello(p, lax.rem(k + i, 8))
 
-    @pl.when(k != cp)
+    def direct(i):
+        return lax.rem(cp + i, 8) * 2 + c
+
+    def relayed(x):
+        return (2 * x + zh) * 2 + c
+
+    @pl.when(outer)
+    def _():
+        for i in (2, 4, 6):
+            hello(direct(i), cp)
+        for x in range(4):
+            hello(relayed(x), cp_flip)
+        hello(p_flip, k_flip)
+
+    @pl.when(jnp.logical_not(outer))
+    def _():
+        for i in range(1, 8):
+            hello(direct(i), cp)
+        for y in range(4):
+            hello(2 * (k + 1 - 2 * zl) + c, 2 * y + 1 - zl)
+            hello(2 * k + c, 2 * y + 1 - zl)
+
+    @pl.when(jnp.logical_and(outer, k != cp))
     def _():
         for s in range(8):
             hello(2 * k + c, s)
@@ -154,12 +185,14 @@
     load("wo", wo_h, wo, lsem.at[10])
     load("pair", pair_h, pbm, psem)
 
+    scale = 1.0 / math.sqrt(32.0)
+
     def project(row, rows, queries):
         x = xs[pl.ds(row, rows), :].astype(F32)
         n = normed(x, again[...])
         y = mm(n, wqkv[...])
         if queries:
-            qs[pl.ds(row - HALO, rows), :] = y[:, 0:128].astype(BF16)
+            qs[pl.ds(row - HALO, rows), :] = (y[:, 0:128] * scale).astype(BF16)
         kf[pl.ds(row, rows), :] = y[:, 128:256].astype(BF16).astype(F32)
         vf[pl.ds(row, rows), :] = y[:, 256:384].astype(BF16).astype(F32)
 
@@ -173,9 +206,66 @@
 
     lax.fori_loop(0, AR // 384, project_own, 0)
 
-    greeted = 14 + jnp.where(p > 0, 1, 0) + jnp.where(p < last, 1, 0) + jnp.where(k != cp, 8, 0)
+    copies["abias"].wait()
+    copies["proj"].wait()
+
+    head_mask = jnp.where(
+        (iota((128, 128), 0) >> 5) == (iota((128, 128), 1) >> 5), 1.0, 0.0
+    ).astype(BF16)
+    lane_head = iota((WQ, 128), 1) >> 5
+    ones = jnp.ones((WK, 128), BF16)
+
+    def by_head(o):
+        return jnp.where(
+            lane_head == 0,
+            o[0:32],
+            jnp.where(lane_head == 1, o[32:64], jnp.where(lane_head == 2, o[64:96], o[96:128])),
+        )
+
+    def scores(b, masked):
+        base = pl.multiple_of(b * WQ, WQ)
+        first = base + jnp.clip(shift_ref[b], -HALO, WQ - HALO)
+        kw = kf[pl.ds(first + HALO, WK), :].astype(BF16)
+        q = qs[pl.ds(base, WQ), :]
+        q4 = jnp.concatenate([q, q, q, q], axis=0) * head_mask
+        s = mm(q4, kw, NT) + ab[:, pl.ds(base, WQ), :].reshape(128, WK).astype(F32)
+        if masked:
+            j = first + p * AR + iota((1, WK), 1)
+            s = jnp.where((j >= 0) & (j < AR * 16), s, -1e30)
+        return base, first, s
+
+    def windows(lo, hi, masked):
+        def group(g, carry):
+            part = [scores(g * UNROLL + u, masked) for u in range(UNROLL)]
+            tops = [jnp.max(s, axis=-1, keepdims=True) for _, _, s in part]
+            weights = [jnp.exp(s - t).astype(BF16) for (_, _, s), t in zip(part, tops)]
+            mixes = []
+            for (_, first, _), w in zip(part, weights):
+                vw = vf[pl.ds(first + HALO, WK), :].astype(BF16)
+                mixes.append(mm(w, jnp.concatenate([vw, ones], axis=1)))
+            for (base, _, _), o in zip(part, mixes):
+                ms[pl.ds(base, WQ), :] = (
+                    by_head(o[:, 0:128]) / by_head(o[:, 128:256])
+                ).astype(BF16)
+            return carry
+
+        lax.fori_loop(lo // UNROLL, hi // UNROLL, group, 0)
+
+    def finish_rows(row, rows):
+        r = pl.ds(row, rows)
+        y = xs[pl.ds(row + HALO, rows), :].astype(F32) + mm(ms[r, :], wproj[...])
+        ao[r, :] = y.astype(BF16)
+
+    windows(24, 56, False)
+
+    greeted = (
+        14
+        + jnp.where(p > 0, 1, 0)
+        + jnp.where(p < last, 1, 0)
+        + jnp.where(k != cp, 8, 0)
+        + jnp.where(outer, 1, 0)
+    )
     pl.semaphore_wait(barrier, greeted)
-
     right = jnp.minimum(p + 1, last)
     left = jnp.maximum(p - 1, 0)
     to_right = send(
@@ -200,55 +290,7 @@
     def _():
         to_left.start()
 
-    copies["abias"].wait()
-    copies["proj"].wait()
-
-    head_mask = jnp.where(
-        (iota((128, 128), 0) >> 5) == (iota((128, 128), 1) >> 5), 1.0, 0.0
-    ).astype(BF16)
-    lane_head = iota((WQ, 128), 1) >> 5
-    ones = jnp.ones((WK, 128), BF16)
-    scale = 1.0 / math.sqrt(32.0)
-
-    def by_head(o):
-        return jnp.where(
-            lane_head == 0,
-            o[0:32],
-            jnp.where(lane_head == 1, o[32:64], jnp.where(lane_head == 2, o[64:96], o[96:128])),
-        )
-
-    def window(b, masked):
-        base = pl.multiple_of(b * WQ, WQ)
-        first = base + jnp.clip(shift_ref[b], -HALO, WQ - HALO)
-        kw = kf[pl.ds(first + HALO, WK), :].astype(BF16)
-        vw = vf[pl.ds(first + HALO, WK), :].astype(BF16)
-        q = qs[pl.ds(base, WQ), :]
-        q4 = jnp.concatenate([q, q, q, q], axis=0) * head_mask
-        s = mm(q4, kw, NT) * scale
-        bias = ab[:, pl.ds(base, WQ), :].reshape(128, WK).astype(F32)
-        s = s + bias
-        if masked:
-            j = first + p * AR + iota((1, WK), 1)
-            s = jnp.where((j >= 0) & (j < AR * 16), s, -1e30)
-        top = jnp.max(s, axis=-1, keepdims=True)
-        w = jnp.exp(s - top).astype(BF16)
-        o = mm(w, jnp.concatenate([vw, ones], axis=1))
-        ms[pl.ds(base, WQ), :] = (by_head(o[:, 0:128]) / by_head(o[:, 128:256])).astype(BF16)
-
-    def windows(lo, hi, masked):
-        def group(g, carry):
-            for u in range(UNROLL):
-                window(g * UNROLL + u, masked)
-            return carry
-
-        lax.fori_loop(lo // UNROLL, hi // UNROLL, group, 0)
-
-    def finish_rows(row, rows):
-        r = pl.ds(row, rows)
-        y = xs[pl.ds(row + HALO, rows), :].astype(F32) + mm(ms[r, :], wproj[...])
-        ao[r, :] = y.astype(BF16)
-
-    windows(24, 84, False)
+    windows(56, 80, False)
 
     @pl.when(p > 0)
     def _():
@@ -268,7 +310,7 @@
 
     project(0, HALO, False)
     project(HALO + AR, HALO, False)
-    windows(84, 96, True)
+    windows(80, 96, True)
     finish_rows(AR - TAIL, TAIL)
 
     @pl.when(p < last)
@@ -290,22 +332,18 @@
     copies["tgain"].wait()
     first_token = p * TR
 
-    def pool(row, rows):
-        v = mm(ao[pl.ds(row, rows), :], wagg[...])
-        hidden = (0.5 * v * (1.0 + jnp.tanh(0.5 * v))).astype(BF16)
+    def slots(row, rows):
         local = ids[:, pl.ds(row, rows)] - first_token
-        hot = jnp.where(local == iota((TR, rows), 0), 1.0, 0.0)
-        acc[...] += mm(hot.astype(BF16), hidden)
-        osc[:, 0:128] += jnp.broadcast_to(jnp.sum(hot, axis=1, keepdims=True), (TR, 128))
-
-    acc[...] = jnp.zeros((TR, CT), F32)
-    osc[:, 0:128] = jnp.zeros((TR, 128), F32)
-
-    def pool_own(i, carry):
-        pool(pl.multiple_of(i * 768, 128), 768)
+        hits = jnp.where(local == iota((TR, rows), 0), 1.0, 0.0)
+        hot[:, pl.ds(row, rows)] = hits.astype(BF16)
+        mlb[...] += hits[:, 0:128] + hits[:, 128:256] + hits[:, 256:384]
+
+    def slots_own(i, carry):
+        slots(pl.multiple_of(i * 384, 128), 384)
         return carry
 
-    lax.fori_loop(0, AR // 768, pool_own, 0)
+    mlb[...] = jnp.zeros((TR, 128), F32)
+    lax.fori_loop(0, AR // 384, slots_own, 0)
 
     @pl.when(p > 0)
     def _():
@@ -317,97 +355,181 @@
         ids[:, pl.ds(AR, TAIL)] = jnp.full((1, TAIL), -1, I32)
         ao[pl.ds(AR, TAIL), :] = jnp.zeros((TAIL, 128), BF16)
 
-    pool(AR, TAIL)
-    repr_f = (acc[...] / osc[:, 0:1]).astype(BF16)
-    rep[...] = repr_f
-    nrm[...] = normed(repr_f.astype(F32), tgain[...])
+    slots(AR, TAIL)
+    counts = jnp.sum(mlb[...], axis=1, keepdims=True)
 
     def rows48(i):
         return pl.ds(pl.multiple_of(i * PIECE, 16), PIECE)
 
+    def landing(core, source):
+        return pl.ds(pl.multiple_of(core * TR + source * PIECE, 16), PIECE)
+
     def half(i):
         return pl.ds(pl.multiple_of(i * TR, 16), TR)
 
-    outs = []
-    for i in range(1, 8):
-        target = lax.rem(cp + i, 8) * 2 + c
-        outs.append(
-            send(
-                nrm.at[rows48(k)],
-                kt.at[pl.ds(pl.multiple_of(c * TR + k * PIECE, 16), PIECE)],
-                xsem.at[i],
-                xrsem.at[k],
-                target,
-                cp,
-            )
+    directs, hops, onward = [], [], []
+    for f, col in enumerate(FEATURES):
+        cols = pl.ds(col, 256)
+        directs.append(
+            [
+                send(
+                    rep.at[rows48(k), cols],
+                    kt.at[landing(c, k), cols],
+                    xsem.at[f, i],
+                    xrsem.at[f, k],
+                    direct(i),
+                    cp,
+                )
+                for i in range(1, 8)
+            ]
         )
-        outs[-1].start()
-
+        hops.append(
+            send(rep.at[rows48(k), cols], rly.at[:, cols], rls.at[f], rlr.at[f], p_flip, k_flip)
+        )
+        onward.append(
+            [
+                send(
+                    rly.at[:, cols],
+                    kt.at[landing(c, k_flip), cols],
+                    rfs.at[f, x],
+                    xrsem.at[f, k_flip],
+                    relayed(x),
+                    cp_flip,
+                )
+                for x in range(4)
+            ]
+        )
+
+    def pass_on(f):
+        @pl.when(outer)
+        def _():
+            hops[f].wait_recv()
+            for copy in onward[f]:
+                copy.start()
+
+    for f, col in enumerate(FEATURES):
+        cols = pl.ds(col, 256)
+
+        def hidden(i, carry):
+            r = pl.ds(pl.multiple_of(i * 384, 128), 384)
+            v = mm(ao[r, :], wagg[:, cols])
+            hid[r, :] = (0.5 * v * (1.0 + jnp.tanh(0.5 * v))).astype(BF16)
+            return carry
+
+        lax.fori_loop(0, (AR + TAIL) // 384, hidden, 0)
+        rep[:, cols] = (mm(hot[...], hid[...]) / counts).astype(BF16)
+
+        @pl.when(outer)
+        def _():
+            for i in (2, 4, 6):
+                directs[f][i - 1].start()
+            hops[f].start()
+
+        @pl.when(jnp.logical_not(outer))
+        def _():
+            for copy in directs[f]:
+                copy.start()
+
+        if f > 0:
+            pass_on(f - 1)
+
+    tscale = 1.0 / math.sqrt(float(HD))
     copies["wq"].wait()
-    qt[...] = mm(nrm[...], wq[...]).astype(BF16)
+    nrm[...] = normed(rep[...].astype(F32), tgain[...].reshape(1, CT))
+    pass_on(len(FEATURES) - 1)
+    qt[...] = (mm(nrm[...], wq[...]) * tscale).astype(BF16)
+    partner = p + 1 - 2 * c
 
     @pl.when(k == cp)
     def _():
-        kt[half(c), :] = nrm[...]
-
-    @pl.when(k != cp)
-    def _():
-        for s in range(8):
-            send(
-                nrm.at[rows48(0)],
-                kt.at[pl.ds(pl.multiple_of(c * TR + s * PIECE, 16), PIECE)],
-                xsem.at[0],
-                xrsem.at[s],
-                p,
-                k,
-            ).wait_recv()
-
-    partner = p + 1 - 2 * c
-    fwd = send(kt.at[half(c)], kt.at[half(c)], fs, fr, partner, k)
-    fwd.start()
+        kt[half(c), :] = rep[...]
+
+    fwds, backs = [], []
+    for f, col in enumerate(FEATURES):
+        cols = pl.ds(col, 256)
+        fwds.append(
+            send(kt.at[half(c), cols], kt.at[half(c), cols], fs.at[f], fr.at[f], partner, k)
+        )
+        backs.append(
+            send(kt.at[half(c), cols], kt.at[half(1 - c), cols], fs.at[f], fr.at[f], partner, k)
+        )
+
+        @pl.when(k != cp)
+        def _():
+            for s in range(8):
+                send(
+                    rep.at[rows48(0), cols],
+                    kt.at[landing(c, s), cols],
+                    xsem.at[f, 0],
+                    xrsem.at[f, s],
+                    partner,
+                    k,
+                ).wait_recv()
+
+        fwds[f].start()
+
     copies["wkv"].wait()
-    back = send(kt.at[half(c)], kt.at[half(1 - c)], fs, fr, partner, k)
-    back.wait_recv()
+    for copy in backs:
+        copy.wait_recv()
+
+    def key_norm(i, carry):
+        r = pl.ds(pl.multiple_of(i * 128, 128), 128)
+        kn[r, :] = normed(kt[r, :].astype(F32), tgain[...].reshape(1, CT))
+        return carry
+
+    lax.fori_loop(0, 2 * TR // 128, key_norm, 0)
 
     def keyvals(j, carry):
         cols = pl.ds(pl.multiple_of(j * 256, 256), 256)
-        kk[:, cols] = mm(kt[...], wkv[:, cols]).astype(BF16)
+        kk[:, cols] = mm(kn[...], wkv[:, cols]).astype(BF16)
         vcols = pl.ds(pl.multiple_of(j * 256 + CT, 256), 256)
-        vv[:, cols] = mm(kt[...], wkv[:, vcols]).astype(BF16)
+        vv[:, cols] = mm(kn[...], wkv[:, vcols]).astype(BF16)
         return carry
 
     lax.fori_loop(0, CT // 256, keyvals, 0)
     copies["pair"].wait()
-    tscale = 1.0 / math.sqrt(float(HD))
     rb = 128
-
-    def head(h, carry):
-        tile = jnp.minimum(lax.div(h * HD, 128), 4)
-        lane0 = pl.multiple_of(tile * 128, 128)
-        off = h * HD - lane0
-        lanes = pl.ds(lane0, 256)
-        keys = kk[:, lanes]
-        values = vv[:, lanes]
-        lane = iota((rb, 256), 1)
-        mask = (lane >= off) & (lane < off + HD)
-        l128 = iota((rb, 128), 1)
-        for r in range(TR // rb):
-            rows = pl.ds(r * rb, rb)
-            q = jnp.where(mask, qt[rows, lanes].astype(F32), 0.0).astype(BF16)
-            s = mm(q, keys, NT) * tscale + pbm[h, rows, :].astype(F32)
+    l128 = iota((rb, 128), 1)
+
+    def heads(pair, carry):
+        work = []
+        for u in range(2):
+            h = pair * 2 + u
+            lane0 = pl.multiple_of(jnp.minimum(lax.div(h * HD, 128), 4) * 128, 128)
+            off = h * HD - lane0
+            lanes = pl.ds(lane0, 256)
+            lane = iota((1, 256), 1)
+            mask = (lane >= off) & (lane < off + HD)
+            values = jnp.where(mask, vv[:, lanes].astype(F32), 1.0).astype(BF16)
+            for r in range(TR // rb):
+                work.append((h, lanes, mask, values, pl.ds(r * rb, rb)))
+
+        def score(h, lanes, mask, values, r):
+            q = jnp.where(mask, qt[r, lanes].astype(F32), 0.0).astype(BF16)
+            return mm(q, kk[:, lanes], NT) + pbm[h, r, :].astype(F32)
+
+        def store(h, lanes, mask, r, top, o):
+            osc[r, lanes] = jnp.where(mask, o, osc[r, lanes])
+            total = jnp.where(mask[:, 0:128], o[:, 128:256], o[:, 0:128])
+            mlb[r, :] = jnp.where(l128 == h, top, jnp.where(l128 == h + TH, total, mlb[r, :]))
+
+        ahead = score(*work[0])
+        done = None
+        for n, (h, lanes, mask, values, r) in enumerate(work):
+            s = ahead
+            if n + 1 < len(work):
+                ahead = score(*work[n + 1])
             top = jnp.max(s, axis=-1, keepdims=True)
-            e = jnp.exp(s - top)
-            total = jnp.sum(e, axis=-1, keepdims=True)
-            o = mm(e.astype(BF16), values)
-            osc[rows, lanes] = jnp.where(mask, o, osc[rows, lanes])
-            mlb[rows, :] = jnp.where(
-                l128 == h, top, jnp.where(l128 == h + TH, total, mlb[rows, :])
-            )
+            o = mm(jnp.exp(s - top).astype(BF16), values)
+            if done is not None:
+                store(*done)
+            done = (h, lanes, mask, r, top, o)
+        store(*done)
         return carry
 
     sends = []
     for n, (lo, hi, col) in enumerate(CHUNKS):
-        lax.fori_loop(lo, hi, head, 0)
+        lax.fori_loop(lo // 2, hi // 2, heads, 0)
         cols = pl.ds(col, 256)
         mixb[:, cols] = osc[:, cols].astype(BF16)
         for i in range(1, 8):
@@ -462,9 +584,23 @@
     for i in range(1, 8):
         src = lax.rem(k + 8 - i, 8)
         send(obuf, tout_h.at[rows48(src)], gs.at[i], gr.at[i], p, src).wait_recv()
-    for copy in gathers + sends + outs:
+    for copy in gathers + sends + fwds:
         copy.wait_send()
-    fwd.wait_send()
+
+    @pl.when(outer)
+    def _():
+        for f in range(len(FEATURES)):
+            for i in (2, 4, 6):
+                directs[f][i - 1].wait_send()
+            hops[f].wait_send()
+            for copy in onward[f]:
+                copy.wait_send()
+
+    @pl.when(jnp.logical_not(outer))
+    def _():
+        for f in range(len(FEATURES)):
+            for copy in directs[f]:
+                copy.wait_send()
 
     @pl.when(p < last)
     def _():
@@ -511,7 +647,7 @@
             vm((4, AR, WK), BF16),
             vm((1, AR + TAIL), I32),
             vm((128, CT), BF16),
-            vm((1, CT), F32),
+            vm((CT,), F32),
             vm((CT, CT), BF16),
             vm((CT, 2 * CT), BF16),
             vm((CT, CT), BF16),
@@ -521,7 +657,10 @@
             vm((EXT, 128), F32),
             vm((AR, 128), BF16),
             vm((AR + TAIL, 128), BF16),
-            vm((TR, CT), F32),
+            vm((TR, AR + TAIL), BF16),
+            vm((AR + TAIL, 256), BF16),
+            vm((PIECE, CT), BF16),
+            vm((2 * TR, CT), BF16),
             vm((TR, CT), BF16),
             vm((TR, CT), BF16),
             vm((TR, CT), BF16),
@@ -539,10 +678,13 @@
             dma((2,)),
             dma((4,)),
             dma((4,)),
-            dma((8,)),
-            dma((8,)),
-            dma,
-            dma,
+            dma((3, 8)),
+            dma((3, 8)),
+            dma((3,)),
+            dma((3,)),
+            dma((3, 4)),
+            dma((3,)),
+            dma((3,)),
             dma((4, 8)),
             dma((4, 8)),
             dma((8,)),
@@ -560,7 +702,7 @@
         atom_bias,
         token_of_atom.reshape(1, AR),
         agg_weight,
-        token_gain.reshape(1, CT),
+        token_gain,
         token_q,
         token_kv,
         token_o,

time: 110 us -> 79.1 us (0.72)
  Pallas kernels: 102 us -> 73.6 us
  local copies, waits for them, and re-layouts: 5.25 us -> 3.98 us
    pallas_call x1, Pallas kernels: 102 us -> 73.6 us  [body(): pl.pallas_call(kernel, out_shape=(jax.ShapeDtypeStruct((AR, 128), BF16),...]
    reshape x1 -> x0, local copies, waits for them, and re-layouts: 1.27 us -> none  [body(): token_gain.reshape(1, CT)]
where the time goes in v2:
time: 79.1 us; the launch traced here: 78.2 us
  Pallas kernels  73.6 us (93%)
  local copies, waits for them, and re-layouts  3.98 us (5%)
    pallas_call x1, Pallas kernels, body(): pl.pallas_call(kernel, out_shape=(jax.ShapeDtypeStruct((AR, 128), BF16),...  73.6 us
    unnamed x2, local copies, waits for them, and re-layouts  3.98 us

profile of v2, /device:TPU:0, one launch (start us, length us, event | category | flops | bytes accessed | tf_op | source)
XLA Modules:
  0.0 78.2 jit_solution(9110935996638888910)
XLA Ops:
  0.6 73.6 %shard_map.140 = (bf16[3072,128]{1,0:T(8,128)(2,1)}, bf16[384,768]{1,0:T(8,128)(2,1)}) custom-call(s32[96]{0:T(128)} %shift_ref.1, bf16[3072,128]{1,0:T(8,128)(2,1)} %atoms_h.1, f32[1,128]{1,0:T(1,128)} %bitcast.3, bf16[128,384]{1,0:T(8,128)(2,1)} %qkv_h.1, bf16[128,128]{1,0:T(8,128)(2,1)} %proj_h.1, bf16[4,3072,128]{2,1,0:T(8,128)(2,1)} %abias_h.1, ...), custom_call_target="tpu_custom_call" | custom-call | tf_op jit(solution)/shard_map/pallas_call | solution.py:634
  74.2 2.1 %copy.17 = bf16[3072,128]{1,0:T(8,128)(2,1)} copy(bf16[3072,128]{1,0:T(8,128)(2,1)} %get-tuple-element.4) | data formatting | bytes 1572864
  76.3 1.9 %copy.18 = bf16[384,768]{1,0:T(8,128)(2,1)} copy(bf16[384,768]{1,0:T(8,128)(2,1)} %get-tuple-element.5) | data formatting | bytes 1179648

commit v3 on v2

--- a/solution.py
+++ b/solution.py
@@ -13,9 +13,10 @@
 EXT = AR + 2 * HALO
 TR, CT, TH, HD = 384, 768, 16, 48
 PIECE = TR // 8
+PARTS = ((0, 256), (256, 128))
 WINDOWS = AR // WQ
 UNROLL = 8
-CHUNKS = ((0, 6, 0), (6, 12, 256), (12, 16, 512))
+CHUNKS = (((0, 8, 0, 384), (8, 14, 384, 256), (14, 16, 640, 128)), ((0, 8, 0, 384), (8, 16, 384, 384)))
 FEATURES = (0, 256, 512)
 NT = (((1,), (1,)), ((), ()))
 NN = (((1,), (0,)), ((), ()))
@@ -82,9 +83,14 @@
     osc,
     mlb,
     mixb,
-    rbuf,
-    rml,
-    obuf,
+    rbuf_a,
+    rbuf_b,
+    mlp_a,
+    mlp_b,
+    rml_a,
+    rml_b,
+    obuf_a,
+    obuf_b,
     lsem,
     psem,
     osem,
@@ -102,6 +108,7 @@
     gs,
     gr,
 ):
+    rbuf, mlp, rml, obuf = (rbuf_a, rbuf_b), (mlp_a, mlp_b), (rml_a, rml_b), (obuf_a, obuf_b)
     p = lax.axis_index("pb")
     k = lax.axis_index("ka")
     c = lax.rem(p, 2)
@@ -256,7 +263,7 @@
         y = xs[pl.ds(row + HALO, rows), :].astype(F32) + mm(ms[r, :], wproj[...])
         ao[r, :] = y.astype(BF16)
 
-    windows(24, 56, False)
+    windows(8, 64, False)
 
     greeted = (
         14
@@ -290,7 +297,7 @@
     def _():
         to_left.start()
 
-    windows(56, 80, False)
+    windows(64, 80, False)
 
     @pl.when(p > 0)
     def _():
@@ -317,7 +324,7 @@
     def _():
         tail_right.start()
 
-    windows(0, 24, True)
+    windows(0, 8, True)
 
     def finish(i, carry):
         finish_rows(pl.multiple_of(i * 384, 384), 384)
@@ -345,18 +352,18 @@
     mlb[...] = jnp.zeros((TR, 128), F32)
     lax.fori_loop(0, AR // 384, slots_own, 0)
 
-    @pl.when(p > 0)
-    def _():
-        ids_right.wait_recv()
-        tail_right.wait_recv()
-
-    @pl.when(p == 0)
-    def _():
-        ids[:, pl.ds(AR, TAIL)] = jnp.full((1, TAIL), -1, I32)
-        ao[pl.ds(AR, TAIL), :] = jnp.zeros((TAIL, 128), BF16)
-
-    slots(AR, TAIL)
-    counts = jnp.sum(mlb[...], axis=1, keepdims=True)
+    def tail_rows():
+        @pl.when(p > 0)
+        def _():
+            ids_right.wait_recv()
+            tail_right.wait_recv()
+
+        @pl.when(p == 0)
+        def _():
+            ids[:, pl.ds(AR, TAIL)] = jnp.full((1, TAIL), -1, I32)
+            ao[pl.ds(AR, TAIL), :] = jnp.zeros((TAIL, 128), BF16)
+
+        slots(AR, TAIL)
 
     def rows48(i):
         return pl.ds(pl.multiple_of(i * PIECE, 16), PIECE)
@@ -411,12 +418,18 @@
         cols = pl.ds(col, 256)
 
         def hidden(i, carry):
-            r = pl.ds(pl.multiple_of(i * 384, 128), 384)
+            r = pl.ds(i * 384 if isinstance(i, int) else pl.multiple_of(i * 384, 128), 384)
             v = mm(ao[r, :], wagg[:, cols])
             hid[r, :] = (0.5 * v * (1.0 + jnp.tanh(0.5 * v))).astype(BF16)
             return carry
 
-        lax.fori_loop(0, (AR + TAIL) // 384, hidden, 0)
+        if f == 0:
+            lax.fori_loop(0, AR // 384, hidden, 0)
+            tail_rows()
+            hidden(AR // 384, 0)
+            counts = jnp.sum(mlb[...], axis=1, keepdims=True)
+        else:
+            lax.fori_loop(0, (AR + TAIL) // 384, hidden, 0)
         rep[:, cols] = (mm(hot[...], hid[...]) / counts).astype(BF16)
 
         @pl.when(outer)
@@ -490,101 +503,148 @@
     copies["pair"].wait()
     rb = 128
     l128 = iota((rb, 128), 1)
-
-    def heads(pair, carry):
-        work = []
-        for u in range(2):
-            h = pair * 2 + u
-            lane0 = pl.multiple_of(jnp.minimum(lax.div(h * HD, 128), 4) * 128, 128)
-            off = h * HD - lane0
-            lanes = pl.ds(lane0, 256)
-            lane = iota((1, 256), 1)
-            mask = (lane >= off) & (lane < off + HD)
-            values = jnp.where(mask, vv[:, lanes].astype(F32), 1.0).astype(BF16)
-            for r in range(TR // rb):
-                work.append((h, lanes, mask, values, pl.ds(r * rb, rb)))
-
-        def score(h, lanes, mask, values, r):
-            q = jnp.where(mask, qt[r, lanes].astype(F32), 0.0).astype(BF16)
-            return mm(q, kk[:, lanes], NT) + pbm[h, r, :].astype(F32)
-
-        def store(h, lanes, mask, r, top, o):
-            osc[r, lanes] = jnp.where(mask, o, osc[r, lanes])
-            total = jnp.where(mask[:, 0:128], o[:, 128:256], o[:, 0:128])
-            mlb[r, :] = jnp.where(l128 == h, top, jnp.where(l128 == h + TH, total, mlb[r, :]))
-
-        ahead = score(*work[0])
-        done = None
-        for n, (h, lanes, mask, values, r) in enumerate(work):
-            s = ahead
-            if n + 1 < len(work):
-                ahead = score(*work[n + 1])
-            top = jnp.max(s, axis=-1, keepdims=True)
-            o = mm(jnp.exp(s - top).astype(BF16), values)
-            if done is not None:
-                store(*done)
-            done = (h, lanes, mask, r, top, o)
-        store(*done)
-        return carry
-
-    sends = []
-    for n, (lo, hi, col) in enumerate(CHUNKS):
-        lax.fori_loop(lo // 2, hi // 2, heads, 0)
-        cols = pl.ds(col, 256)
-        mixb[:, cols] = osc[:, cols].astype(BF16)
+    copies["wo"].wait()
+
+    def make_heads(row, rows, together):
+        def heads(group, carry):
+            work = []
+            for u in range(together):
+                h = group * together + u
+                lane0 = pl.multiple_of(jnp.minimum(lax.div(h * HD, 128), 4) * 128, 128)
+                off = h * HD - lane0
+                lanes = pl.ds(lane0, 256)
+                lane = iota((1, 256), 1)
+                mask = (lane >= off) & (lane < off + HD)
+                values = jnp.where(mask, vv[:, lanes].astype(F32), 1.0).astype(BF16)
+                for r in range(row, row + rows, rb):
+                    work.append((h, lanes, mask, values, pl.ds(r, rb)))
+
+            def score(h, lanes, mask, values, r):
+                q = jnp.where(mask, qt[r, lanes].astype(F32), 0.0).astype(BF16)
+                return mm(q, kk[:, lanes], NT) + pbm[h, r, :].astype(F32)
+
+            def store(h, lanes, mask, r, top, o):
+                osc[r, lanes] = jnp.where(mask, o, osc[r, lanes])
+                total = jnp.where(mask[:, 0:128], o[:, 128:256], o[:, 0:128])
+                mlb[r, :] = jnp.where(l128 == h, top, jnp.where(l128 == h + TH, total, mlb[r, :]))
+
+            ahead = score(*work[0])
+            done = None
+            for n, (h, lanes, mask, values, r) in enumerate(work):
+                s = ahead
+                if n + 1 < len(work):
+                    ahead = score(*work[n + 1])
+                top = jnp.max(s, axis=-1, keepdims=True)
+                o = mm(jnp.exp(s - top).astype(BF16), values)
+                if done is not None:
+                    store(*done)
+                done = (h, lanes, mask, r, top, o)
+            store(*done)
+            return carry
+
+        return heads
+
+    i0, j0 = iota((128, CT), 0) * HD, iota((128, CT), 1)
+    expand = jnp.where((j0 >= i0) & (j0 < i0 + HD), 1.0, 0.0).astype(BF16)
+    sends, gathers = ([], []), ([], [])
+
+    def owned(part, owner):
+        row, rows = PARTS[part]
+        return pl.ds(pl.multiple_of(row + owner * (rows // 8), 16), rows // 8)
+
+    def attend(part, n):
+        row, rows = PARTS[part]
+        lo, hi, col, width = CHUNKS[part][n]
+        together = 512 // rows
+        lax.fori_loop(lo // together, hi // together, make_heads(row, rows, together), 0)
+        cols = pl.ds(col, width)
+        mixb[pl.ds(row, rows), cols] = osc[pl.ds(row, rows), cols].astype(BF16)
         for i in range(1, 8):
             peer = lax.rem(k + i, 8)
-            sends.append(
-                send(
-                    mixb.at[rows48(peer), cols],
-                    rbuf.at[i, :, cols],
-                    rs.at[n, i],
-                    rr.at[n, i],
-                    p,
-                    peer,
-                )
+            copy = send(
+                mixb.at[owned(part, peer), cols],
+                rbuf[part].at[i, :, cols],
+                rs.at[part, n, i],
+                rr.at[part, n, i],
+                p,
+                peer,
             )
-            sends[-1].start()
-    for i in range(1, 8):
-        peer = lax.rem(k + i, 8)
-        sends.append(send(mlb.at[rows48(peer)], rml.at[i], rs.at[3, i], rr.at[3, i], p, peer))
-        sends[-1].start()
-
-    rbuf[0, :, :] = mixb[rows48(k), :]
-    rml[0, :, :] = mlb[rows48(k), :]
-    copies["wo"].wait()
-    for copy in sends:
-        copy.wait_recv()
-
-    ml = rml[...]
-    tot = pltpu.roll(ml.reshape(8 * PIECE, 128), 128 - TH, 1).reshape(8, PIECE, 128)
-    real = iota((8, PIECE, 128), 2) < TH
-    ml = jnp.where(real, ml, 0.0)
-    tot = jnp.where(real, tot, 1.0)
-    top = jnp.max(ml, axis=0, keepdims=True)
-    factor = jnp.exp(ml - top)
-    weight = factor / jnp.sum(factor * tot, axis=0, keepdims=True)
-    weight = weight.reshape(8 * PIECE, 128)
-    high = weight.astype(BF16)
-    low = (weight - high.astype(F32)).astype(BF16)
-    i0, j0 = iota((128, CT), 0) * HD, iota((128, CT), 1)
-    expand = jnp.where((j0 >= i0) & (j0 < i0 + HD), 1.0, 0.0).astype(BF16)
-    wide = (mm(high, expand) + mm(low, expand)).reshape(8, PIECE, CT)
-    mix = jnp.sum(wide * rbuf[...].astype(F32), axis=0).astype(BF16)
-    obuf[...] = (rep[rows48(k), :].astype(F32) + mm(mix, wo[...])).astype(BF16)
-    own = pltpu.make_async_copy(obuf, tout_h.at[rows48(k)], osem.at[1])
-    own.start()
-    gathers = []
-    for i in range(1, 8):
-        peer = lax.rem(k + i, 8)
-        gathers.append(send(obuf, tout_h.at[rows48(k)], gs.at[i], gr.at[i], p, peer))
-        gathers[-1].start()
-    own.wait()
+            copy.start()
+            sends[part].append(copy)
+
+    def share_sums(part):
+        row, rows = PARTS[part]
+        count = rows // 64
+        grouped = mlb[pl.ds(row, rows), :].reshape(8, count, 8, 128)
+        lane = iota((8, 8, 128), 2)
+        packed = grouped[:, 0]
+        for j in range(1, count):
+            turned = pltpu.roll(grouped[:, j].reshape(64, 128), 32 * j, 1).reshape(8, 8, 128)
+            packed = jnp.where(lane >= 32 * j, turned, packed)
+        mlp[part][...] = packed
+        for i in range(1, 8):
+            peer = lax.rem(k + i, 8)
+            copy = send(
+                mlp[part].at[peer], rml[part].at[i], rs.at[part, 3, i], rr.at[part, 3, i], p, peer
+            )
+            copy.start()
+            sends[part].append(copy)
+
+    def merge(part):
+        row, rows = PARTS[part]
+        piece, count = rows // 8, rows // 64
+        rbuf[part][0, :, :] = mixb[owned(part, k), :]
+        rml[part][0, :, :] = mlp[part][k, :, :]
+        for copy in sends[part]:
+            copy.wait_recv()
+        packed = rml[part][...].reshape(64, 128)
+        tops, tots = [], []
+        for j in range(count):
+            tops.append(packed if j == 0 else pltpu.roll(packed, 128 - 32 * j, 1))
+            tots.append(pltpu.roll(packed, 128 - 32 * j - TH, 1))
+        ml = jnp.stack([t.reshape(8, 8, 128) for t in tops], axis=1).reshape(8, piece, 128)
+        tot = jnp.stack([t.reshape(8, 8, 128) for t in tots], axis=1).reshape(8, piece, 128)
+        real = iota((8, piece, 128), 2) < TH
+        ml = jnp.where(real, ml, 0.0)
+        tot = jnp.where(real, tot, 1.0)
+        top = jnp.max(ml, axis=0, keepdims=True)
+        factor = jnp.exp(ml - top)
+        weight = factor / jnp.sum(factor * tot, axis=0, keepdims=True)
+        weight = weight.reshape(8 * piece, 128)
+        high = weight.astype(BF16)
+        low = (weight - high.astype(F32)).astype(BF16)
+        wide = (mm(high, expand) + mm(low, expand)).reshape(8, piece, CT)
+        mix = jnp.sum(wide * rbuf[part][...].astype(F32), axis=0).astype(BF16)
+        obuf[part][...] = (rep[owned(part, k), :].astype(F32) + mm(mix, wo[...])).astype(BF16)
+        own = pltpu.make_async_copy(obuf[part], tout_h.at[owned(part, k)], osem.at[1 + part])
+        own.start()
+        for i in range(1, 8):
+            peer = lax.rem(k + i, 8)
+            copy = send(
+                obuf[part], tout_h.at[owned(part, k)], gs.at[part, i], gr.at[part, i], p, peer
+            )
+            copy.start()
+            gathers[part].append(copy)
+        return own
+
+    for n in range(len(CHUNKS[0])):
+        attend(0, n)
+    share_sums(0)
+    attend(1, 0)
+    own_a = merge(0)
+    attend(1, 1)
+    share_sums(1)
+    own_b = merge(1)
+    own_a.wait()
+    own_b.wait()
     aout_copy.wait()
-    for i in range(1, 8):
-        src = lax.rem(k + 8 - i, 8)
-        send(obuf, tout_h.at[rows48(src)], gs.at[i], gr.at[i], p, src).wait_recv()
-    for copy in gathers + sends + fwds:
+    for part in range(2):
+        for i in range(1, 8):
+            src = lax.rem(k + 8 - i, 8)
+            send(
+                obuf[part], tout_h.at[owned(part, src)], gs.at[part, i], gr.at[part, i], p, src
+            ).wait_recv()
+    for copy in gathers[0] + gathers[1] + sends[0] + sends[1] + fwds:
         copy.wait_send()
 
     @pl.when(outer)
@@ -670,12 +730,17 @@
             vm((TR, CT), F32),
             vm((TR, 128), F32),
             vm((TR, CT), BF16),
-            vm((8, PIECE, CT), BF16),
-            vm((8, PIECE, 128), F32),
-            vm((PIECE, CT), BF16),
+            vm((8, 32, CT), BF16),
+            vm((8, 16, CT), BF16),
+            vm((8, 8, 128), F32),
+            vm((8, 8, 128), F32),
+            vm((8, 8, 128), F32),
+            vm((8, 8, 128), F32),
+            vm((32, CT), BF16),
+            vm((16, CT), BF16),
             dma((11,)),
             dma,
-            dma((2,)),
+            dma((3,)),
             dma((4,)),
             dma((4,)),
             dma((3, 8)),
@@ -685,10 +750,10 @@
             dma((3, 4)),
             dma((3,)),
             dma((3,)),
-            dma((4, 8)),
-            dma((4, 8)),
-            dma((8,)),
-            dma((8,)),
+            dma((2, 4, 8)),
+            dma((2, 4, 8)),
+            dma((2, 8)),
+            dma((2, 8)),
         ],
         compiler_params=pltpu.CompilerParams(
             collective_id=0, has_side_effects=True, vmem_limit_bytes=60 * 1024 * 1024

time: 79.1 us -> 79.4 us (level)
  Pallas kernels: 73.6 us -> 74.6 us
    pallas_call x1, Pallas kernels: 73.6 us -> 74.6 us  [body(): pl.pallas_call(kernel, out_shape=(jax.ShapeDtypeStruct((AR, 128), BF16),...]
where the time goes in v3:
time: 79.4 us; the launch traced here: 79.2 us
  Pallas kernels  74.6 us (94%)
  local copies, waits for them, and re-layouts  3.98 us (5%)
    pallas_call x1, Pallas kernels, body(): pl.pallas_call(kernel, out_shape=(jax.ShapeDtypeStruct((AR, 128), BF16),...  74.6 us
    unnamed x2, local copies, waits for them, and re-layouts  3.98 us

profile of v3, /device:TPU:0, one launch (start us, length us, event | category | flops | bytes accessed | tf_op | source)
XLA Modules:
  0.0 79.2 jit_solution(15236336587041652358)
XLA Ops:
  0.6 74.6 %shard_map.140 = (bf16[3072,128]{1,0:T(8,128)(2,1)}, bf16[384,768]{1,0:T(8,128)(2,1)}) custom-call(s32[96]{0:T(128)} %shift_ref.1, bf16[3072,128]{1,0:T(8,128)(2,1)} %atoms_h.1, f32[1,128]{1,0:T(1,128)} %bitcast.3, bf16[128,384]{1,0:T(8,128)(2,1)} %qkv_h.1, bf16[128,128]{1,0:T(8,128)(2,1)} %proj_h.1, bf16[4,3072,128]{2,1,0:T(8,128)(2,1)} %abias_h.1, ...), custom_call_target="tpu_custom_call" | custom-call | tf_op jit(solution)/shard_map/pallas_call | solution.py:694
  75.2 2.1 %copy.17 = bf16[3072,128]{1,0:T(8,128)(2,1)} copy(bf16[3072,128]{1,0:T(8,128)(2,1)} %get-tuple-element.4) | data formatting | bytes 1572864
  77.3 1.9 %copy.18 = bf16[384,768]{1,0:T(8,128)(2,1)} copy(bf16[384,768]{1,0:T(8,128)(2,1)} %get-tuple-element.5) | data formatting | bytes 1179648

commit v4 on v3

--- a/solution.py
+++ b/solution.py
@@ -135,6 +135,15 @@
             device_id_type=pl.DeviceIdType.MESH,
         )
 
+    copies = {}
+
+    def load(name, src, dst, sem):
+        copies[name] = pltpu.make_async_copy(src, dst, sem)
+        copies[name].start()
+
+    load("atoms", atoms_h, xs.at[pl.ds(HALO, AR)], lsem.at[0])
+    load("again", again_h, again, lsem.at[1])
+    load("qkv", qkv_h, wqkv, lsem.at[2])
     @pl.when(p > 0)
     def _():
         hello(p - 1, k)
@@ -173,15 +182,6 @@
         for s in range(8):
             hello(2 * k + c, s)
 
-    copies = {}
-
-    def load(name, src, dst, sem):
-        copies[name] = pltpu.make_async_copy(src, dst, sem)
-        copies[name].start()
-
-    load("atoms", atoms_h, xs.at[pl.ds(HALO, AR)], lsem.at[0])
-    load("again", again_h, again, lsem.at[1])
-    load("qkv", qkv_h, wqkv, lsem.at[2])
     load("abias", abias_h, ab, lsem.at[3])
     load("proj", proj_h, wproj, lsem.at[4])
     load("agg", agg_h, wagg, lsem.at[5])
@@ -194,24 +194,26 @@
 
     scale = 1.0 / math.sqrt(32.0)
 
-    def project(row, rows, queries):
-        x = xs[pl.ds(row, rows), :].astype(F32)
-        n = normed(x, again[...])
-        y = mm(n, wqkv[...])
-        if queries:
-            qs[pl.ds(row - HALO, rows), :] = (y[:, 0:128] * scale).astype(BF16)
-        kf[pl.ds(row, rows), :] = y[:, 128:256].astype(BF16).astype(F32)
-        vf[pl.ds(row, rows), :] = y[:, 256:384].astype(BF16).astype(F32)
+    def project(parts, rows, queries):
+        outs = [
+            mm(normed(xs[pl.ds(row, rows), :].astype(F32), again[...]), wqkv[...]) for row in parts
+        ]
+        for row, y in zip(parts, outs):
+            if queries:
+                qs[pl.ds(row - HALO, rows), :] = (y[:, 0:128] * scale).astype(BF16)
+            kf[pl.ds(row, rows), :] = y[:, 128:256].astype(BF16).astype(F32)
+            vf[pl.ds(row, rows), :] = y[:, 256:384].astype(BF16).astype(F32)
 
     copies["atoms"].wait()
     copies["again"].wait()
     copies["qkv"].wait()
 
     def project_own(i, carry):
-        project(pl.multiple_of(HALO + i * 384, 64), 384, True)
+        base = HALO + i * 768
+        project([pl.multiple_of(base + u * 256, 64) for u in range(3)], 256, True)
         return carry
 
-    lax.fori_loop(0, AR // 384, project_own, 0)
+    lax.fori_loop(0, AR // 768, project_own, 0)
 
     copies["abias"].wait()
     copies["proj"].wait()
@@ -263,7 +265,38 @@
         y = xs[pl.ds(row + HALO, rows), :].astype(F32) + mm(ms[r, :], wproj[...])
         ao[r, :] = y.astype(BF16)
 
-    windows(8, 64, False)
+    def chunk(i):
+        return i * 384 if isinstance(i, int) else pl.multiple_of(i * 384, 384)
+
+    def hidden(f, parts):
+        cols = pl.ds(FEATURES[f], 256)
+        rows = [pl.ds(chunk(i), 384) for i in parts]
+        outs = [mm(ao[r, :], wagg[:, cols]) for r in rows]
+        for r, v in zip(rows, outs):
+            hid[f, r, :] = (0.5 * v * (1.0 + jnp.tanh(0.5 * v))).astype(BF16)
+
+    def hidden_three(f, lo, hi):
+        def body(g, carry):
+            hidden(f, [g * 3 + u for u in range(3)])
+            return carry
+
+        lax.fori_loop(lo, hi, body, 0)
+
+    def finish(i, carry):
+        finish_rows(chunk(i), 384)
+        return carry
+
+    def slots(row, rows):
+        local = ids[:, pl.ds(row, rows)] - p * TR
+        hits = jnp.where(local == iota((TR, rows), 0), 1.0, 0.0)
+        hot[:, pl.ds(row, rows)] = hits.astype(BF16)
+        mlb[...] += hits[:, 0:128] + hits[:, 128:256] + hits[:, 256:384]
+
+    def slots_own(i, carry):
+        slots(pl.multiple_of(i * 384, 128), 384)
+        return carry
+
+    windows(8, 32, False)
 
     greeted = (
         14
@@ -297,7 +330,14 @@
     def _():
         to_left.start()
 
-    windows(64, 80, False)
+    windows(32, 80, False)
+    copies["ids"].wait()
+    mlb[...] = jnp.zeros((TR, 128), F32)
+    lax.fori_loop(0, AR // 384, slots_own, 0)
+    lax.fori_loop(1, 6, finish, 0)
+    copies["agg"].wait()
+    hidden(0, (1, 2, 3))
+    hidden(0, (4, 5))
 
     @pl.when(p > 0)
     def _():
@@ -315,8 +355,7 @@
     def _():
         xs[pl.ds(HALO + AR, HALO), :] = jnp.zeros((HALO, 128), BF16)
 
-    project(0, HALO, False)
-    project(HALO + AR, HALO, False)
+    project([0, HALO + AR], HALO, False)
     windows(80, 96, True)
     finish_rows(AR - TAIL, TAIL)
 
@@ -326,32 +365,12 @@
 
     windows(0, 8, True)
 
-    def finish(i, carry):
-        finish_rows(pl.multiple_of(i * 384, 384), 384)
-        return carry
-
-    lax.fori_loop(0, (AR - TAIL) // 384, finish, 0)
+    finish(0, 0)
+    finish(6, 0)
     aout_copy = pltpu.make_async_copy(ao.at[pl.ds(0, AR)], aout_h, osem.at[0])
     aout_copy.start()
 
-    copies["agg"].wait()
-    copies["ids"].wait()
     copies["tgain"].wait()
-    first_token = p * TR
-
-    def slots(row, rows):
-        local = ids[:, pl.ds(row, rows)] - first_token
-        hits = jnp.where(local == iota((TR, rows), 0), 1.0, 0.0)
-        hot[:, pl.ds(row, rows)] = hits.astype(BF16)
-        mlb[...] += hits[:, 0:128] + hits[:, 128:256] + hits[:, 256:384]
-
-    def slots_own(i, carry):
-        slots(pl.multiple_of(i * 384, 128), 384)
-        return carry
-
-    mlb[...] = jnp.zeros((TR, 128), F32)
-    lax.fori_loop(0, AR // 384, slots_own, 0)
-
     def tail_rows():
         @pl.when(p > 0)
         def _():
@@ -417,20 +436,21 @@
     for f, col in enumerate(FEATURES):
         cols = pl.ds(col, 256)
 
-        def hidden(i, carry):
-            r = pl.ds(i * 384 if isinstance(i, int) else pl.multiple_of(i * 384, 128), 384)
-            v = mm(ao[r, :], wagg[:, cols])
-            hid[r, :] = (0.5 * v * (1.0 + jnp.tanh(0.5 * v))).astype(BF16)
-            return carry
-
         if f == 0:
-            lax.fori_loop(0, AR // 384, hidden, 0)
+            hidden(0, (0, 6, 7))
+            pooled = mm(hot[:, 0:AR], hid[0, 0:AR, :])
+            hidden_three(1, 0, 2)
+            hidden(1, (6, 7))
             tail_rows()
-            hidden(AR // 384, 0)
+            hidden(0, (8,))
+            hidden(1, (8,))
             counts = jnp.sum(mlb[...], axis=1, keepdims=True)
+            pooled += mm(hot[:, AR : AR + TAIL], hid[0, AR : AR + TAIL, :])
         else:
-            lax.fori_loop(0, (AR + TAIL) // 384, hidden, 0)
-        rep[:, cols] = (mm(hot[...], hid[...]) / counts).astype(BF16)
+            if f == 2:
+                hidden_three(2, 0, 3)
+            pooled = mm(hot[...], hid[f])
+        rep[:, cols] = (pooled / counts).astype(BF16)
 
         @pl.when(outer)
         def _():
@@ -449,8 +469,8 @@
     tscale = 1.0 / math.sqrt(float(HD))
     copies["wq"].wait()
     nrm[...] = normed(rep[...].astype(F32), tgain[...].reshape(1, CT))
+    qt[...] = (mm(nrm[...], wq[...]) * tscale).astype(BF16)
     pass_on(len(FEATURES) - 1)
-    qt[...] = (mm(nrm[...], wq[...]) * tscale).astype(BF16)
     partner = p + 1 - 2 * c
 
     @pl.when(k == cp)
@@ -481,25 +501,24 @@
 
         fwds[f].start()
 
+    def project_half(i):
+        r = half(i)
+        kn[...] = normed(kt[r, :].astype(F32), tgain[...].reshape(1, CT))
+
+        def keyvals(j, carry):
+            cols = pl.ds(pl.multiple_of(j * 256, 256), 256)
+            kk[r, cols] = mm(kn[...], wkv[:, cols]).astype(BF16)
+            vcols = pl.ds(pl.multiple_of(j * 256 + CT, 256), 256)
+            vv[r, cols] = mm(kn[...], wkv[:, vcols]).astype(BF16)
+            return carry
+
+        lax.fori_loop(0, CT // 256, keyvals, 0)
+
     copies["wkv"].wait()
+    project_half(c)
     for copy in backs:
         copy.wait_recv()
-
-    def key_norm(i, carry):
-        r = pl.ds(pl.multiple_of(i * 128, 128), 128)
-        kn[r, :] = normed(kt[r, :].astype(F32), tgain[...].reshape(1, CT))
-        return carry
-
-    lax.fori_loop(0, 2 * TR // 128, key_norm, 0)
-
-    def keyvals(j, carry):
-        cols = pl.ds(pl.multiple_of(j * 256, 256), 256)
-        kk[:, cols] = mm(kn[...], wkv[:, cols]).astype(BF16)
-        vcols = pl.ds(pl.multiple_of(j * 256 + CT, 256), 256)
-        vv[:, cols] = mm(kn[...], wkv[:, vcols]).astype(BF16)
-        return carry
-
-    lax.fori_loop(0, CT // 256, keyvals, 0)
+    project_half(1 - c)
     copies["pair"].wait()
     rb = 128
     l128 = iota((rb, 128), 1)
@@ -515,13 +534,13 @@
                 lanes = pl.ds(lane0, 256)
                 lane = iota((1, 256), 1)
                 mask = (lane >= off) & (lane < off + HD)
-                values = jnp.where(mask, vv[:, lanes].astype(F32), 1.0).astype(BF16)
+                keep = jnp.where(mask, 1.0, 0.0).astype(BF16)
+                values = vv[:, lanes] * keep + (1.0 - keep)
                 for r in range(row, row + rows, rb):
-                    work.append((h, lanes, mask, values, pl.ds(r, rb)))
-
-            def score(h, lanes, mask, values, r):
-                q = jnp.where(mask, qt[r, lanes].astype(F32), 0.0).astype(BF16)
-                return mm(q, kk[:, lanes], NT) + pbm[h, r, :].astype(F32)
+                    work.append((h, lanes, mask, keep, values, pl.ds(r, rb)))
+
+            def score(h, lanes, mask, keep, values, r):
+                return mm(qt[r, lanes] * keep, kk[:, lanes], NT) + pbm[h, r, :].astype(F32)
 
             def store(h, lanes, mask, r, top, o):
                 osc[r, lanes] = jnp.where(mask, o, osc[r, lanes])
@@ -530,7 +549,7 @@
 
             ahead = score(*work[0])
             done = None
-            for n, (h, lanes, mask, values, r) in enumerate(work):
+            for n, (h, lanes, mask, keep, values, r) in enumerate(work):
                 s = ahead
                 if n + 1 < len(work):
                     ahead = score(*work[n + 1])
@@ -631,9 +650,9 @@
         attend(0, n)
     share_sums(0)
     attend(1, 0)
-    own_a = merge(0)
     attend(1, 1)
     share_sums(1)
+    own_a = merge(0)
     own_b = merge(1)
     own_a.wait()
     own_b.wait()
@@ -718,9 +737,9 @@
             vm((AR, 128), BF16),
             vm((AR + TAIL, 128), BF16),
             vm((TR, AR + TAIL), BF16),
-            vm((AR + TAIL, 256), BF16),
+            vm((3, AR + TAIL, 256), BF16),
             vm((PIECE, CT), BF16),
-            vm((2 * TR, CT), BF16),
+            vm((TR, CT), BF16),
             vm((TR, CT), BF16),
             vm((TR, CT), BF16),
             vm((TR, CT), BF16),

time: 79.4 us -> 73.7 us (0.928)
  Pallas kernels: 74.6 us -> 68.9 us
    pallas_call x1, Pallas kernels: 74.6 us -> 68.9 us  [body(): pl.pallas_call(kernel, out_shape=(jax.ShapeDtypeStruct((AR, 128), BF16),...]
where the time goes in v4:
time: 73.7 us; the launch traced here: 73.5 us
  Pallas kernels  68.9 us (93%)
  local copies, waits for them, and re-layouts  3.98 us (5%)
    pallas_call x1, Pallas kernels, body(): pl.pallas_call(kernel, out_shape=(jax.ShapeDtypeStruct((AR, 128), BF16),...  68.9 us
    unnamed x2, local copies, waits for them, and re-layouts  3.98 us

profile of v4, /device:TPU:0, one launch (start us, length us, event | category | flops | bytes accessed | tf_op | source)
XLA Modules:
  0.0 73.5 jit_solution(10693784125838093768)
XLA Ops:
  0.6 68.9 %shard_map.140 = (bf16[3072,128]{1,0:T(8,128)(2,1)}, bf16[384,768]{1,0:T(8,128)(2,1)}) custom-call(s32[96]{0:T(128)} %shift_ref.1, bf16[3072,128]{1,0:T(8,128)(2,1)} %atoms_h.1, f32[1,128]{1,0:T(1,128)} %bitcast.3, bf16[128,384]{1,0:T(8,128)(2,1)} %qkv_h.1, bf16[128,128]{1,0:T(8,128)(2,1)} %proj_h.1, bf16[4,3072,128]{2,1,0:T(8,128)(2,1)} %abias_h.1, ...), custom_call_target="tpu_custom_call" | custom-call | tf_op jit(solution)/shard_map/pallas_call | solution.py:713
  69.5 2.1 %copy.17 = bf16[3072,128]{1,0:T(8,128)(2,1)} copy(bf16[3072,128]{1,0:T(8,128)(2,1)} %get-tuple-element.4) | data formatting | bytes 1572864
  71.6 1.9 %copy.18 = bf16[384,768]{1,0:T(8,128)(2,1)} copy(bf16[384,768]{1,0:T(8,128)(2,1)} %get-tuple-element.5) | data formatting | bytes 1179648

commit v5 on v4

--- a/solution.py
+++ b/solution.py
@@ -72,7 +72,6 @@
     ao,
     hot,
     hid,
-    rly,
     kn,
     rep,
     nrm,
@@ -98,9 +97,6 @@
     hr,
     xsem,
     xrsem,
-    rls,
-    rlr,
-    rfs,
     fs,
     fr,
     rs,
@@ -113,9 +109,6 @@
     k = lax.axis_index("ka")
     c = lax.rem(p, 2)
     cp = lax.div(p, 2)
-    zh, zl = lax.rem(cp, 2), lax.rem(k, 2)
-    outer = zh == zl
-    cp_flip, k_flip, p_flip = cp + 1 - 2 * zh, k + 1 - 2 * zl, p + 2 - 4 * zh
     last = 15
     barrier = pltpu.get_barrier_semaphore()
 
@@ -152,32 +145,14 @@
     def _():
         hello(p + 1, k)
 
+    def direct(i):
+        return lax.rem(cp + i, 8) * 2 + c
+
     for i in range(1, 8):
         hello(p, lax.rem(k + i, 8))
-
-    def direct(i):
-        return lax.rem(cp + i, 8) * 2 + c
-
-    def relayed(x):
-        return (2 * x + zh) * 2 + c
-
-    @pl.when(outer)
-    def _():
-        for i in (2, 4, 6):
-            hello(direct(i), cp)
-        for x in range(4):
-            hello(relayed(x), cp_flip)
-        hello(p_flip, k_flip)
-
-    @pl.when(jnp.logical_not(outer))
-    def _():
-        for i in range(1, 8):
-            hello(direct(i), cp)
-        for y in range(4):
-            hello(2 * (k + 1 - 2 * zl) + c, 2 * y + 1 - zl)
-            hello(2 * k + c, 2 * y + 1 - zl)
-
-    @pl.when(jnp.logical_and(outer, k != cp))
+        hello(direct(i), cp)
+
+    @pl.when(k != cp)
     def _():
         for s in range(8):
             hello(2 * k + c, s)
@@ -296,14 +271,13 @@
         slots(pl.multiple_of(i * 384, 128), 384)
         return carry
 
-    windows(8, 32, False)
+    windows(8, 16, False)
 
     greeted = (
         14
         + jnp.where(p > 0, 1, 0)
         + jnp.where(p < last, 1, 0)
         + jnp.where(k != cp, 8, 0)
-        + jnp.where(outer, 1, 0)
     )
     pl.semaphore_wait(barrier, greeted)
     right = jnp.minimum(p + 1, last)
@@ -330,39 +304,39 @@
     def _():
         to_left.start()
 
-    windows(32, 80, False)
+    windows(16, 80, False)
     copies["ids"].wait()
     mlb[...] = jnp.zeros((TR, 128), F32)
     lax.fori_loop(0, AR // 384, slots_own, 0)
+
+    @pl.when(p > 0)
+    def _():
+        to_right.wait_recv()
+
+    @pl.when(p < last)
+    def _():
+        to_left.wait_recv()
+
+    @pl.when(p == 0)
+    def _():
+        xs[pl.ds(0, HALO), :] = jnp.zeros((HALO, 128), BF16)
+
+    @pl.when(p == last)
+    def _():
+        xs[pl.ds(HALO + AR, HALO), :] = jnp.zeros((HALO, 128), BF16)
+
+    project([0, HALO + AR], HALO, False)
+    windows(80, 96, True)
+    finish_rows(AR - TAIL, TAIL)
+
+    @pl.when(p < last)
+    def _():
+        tail_right.start()
+
     lax.fori_loop(1, 6, finish, 0)
     copies["agg"].wait()
     hidden(0, (1, 2, 3))
     hidden(0, (4, 5))
-
-    @pl.when(p > 0)
-    def _():
-        to_right.wait_recv()
-
-    @pl.when(p < last)
-    def _():
-        to_left.wait_recv()
-
-    @pl.when(p == 0)
-    def _():
-        xs[pl.ds(0, HALO), :] = jnp.zeros((HALO, 128), BF16)
-
-    @pl.when(p == last)
-    def _():
-        xs[pl.ds(HALO + AR, HALO), :] = jnp.zeros((HALO, 128), BF16)
-
-    project([0, HALO + AR], HALO, False)
-    windows(80, 96, True)
-    finish_rows(AR - TAIL, TAIL)
-
-    @pl.when(p < last)
-    def _():
-        tail_right.start()
-
     windows(0, 8, True)
 
     finish(0, 0)
@@ -393,45 +367,17 @@
     def half(i):
         return pl.ds(pl.multiple_of(i * TR, 16), TR)
 
-    directs, hops, onward = [], [], []
-    for f, col in enumerate(FEATURES):
-        cols = pl.ds(col, 256)
-        directs.append(
-            [
-                send(
-                    rep.at[rows48(k), cols],
-                    kt.at[landing(c, k), cols],
-                    xsem.at[f, i],
-                    xrsem.at[f, k],
-                    direct(i),
-                    cp,
-                )
-                for i in range(1, 8)
-            ]
-        )
-        hops.append(
-            send(rep.at[rows48(k), cols], rly.at[:, cols], rls.at[f], rlr.at[f], p_flip, k_flip)
-        )
-        onward.append(
-            [
-                send(
-                    rly.at[:, cols],
-                    kt.at[landing(c, k_flip), cols],
-                    rfs.at[f, x],
-                    xrsem.at[f, k_flip],
-                    relayed(x),
-                    cp_flip,
-                )
-                for x in range(4)
-            ]
-        )
-
-    def pass_on(f):
-        @pl.when(outer)
-        def _():
-            hops[f].wait_recv()
-            for copy in onward[f]:
-                copy.start()
+    def pooled_sends(f):
+        cols = pl.ds(FEATURES[f], 256)
+        for i in range(1, 8):
+            send(
+                rep.at[rows48(k), cols],
+                kt.at[landing(c, k), cols],
+                xsem.at[f],
+                xrsem.at[f],
+                direct(i),
+                cp,
+            ).start()
 
     for f, col in enumerate(FEATURES):
         cols = pl.ds(col, 256)
@@ -452,25 +398,12 @@
             pooled = mm(hot[...], hid[f])
         rep[:, cols] = (pooled / counts).astype(BF16)
 
-        @pl.when(outer)
-        def _():
-            for i in (2, 4, 6):
-                directs[f][i - 1].start()
-            hops[f].start()
-
-        @pl.when(jnp.logical_not(outer))
-        def _():
-            for copy in directs[f]:
-                copy.start()
-
-        if f > 0:
-            pass_on(f - 1)
+        pooled_sends(f)
 
     tscale = 1.0 / math.sqrt(float(HD))
     copies["wq"].wait()
     nrm[...] = normed(rep[...].astype(F32), tgain[...].reshape(1, CT))
     qt[...] = (mm(nrm[...], wq[...]) * tscale).astype(BF16)
-    pass_on(len(FEATURES) - 1)
     partner = p + 1 - 2 * c
 
     @pl.when(k == cp)
@@ -489,15 +422,9 @@
 
         @pl.when(k != cp)
         def _():
-            for s in range(8):
-                send(
-                    rep.at[rows48(0), cols],
-                    kt.at[landing(c, s), cols],
-                    xsem.at[f, 0],
-                    xrsem.at[f, s],
-                    partner,
-                    k,
-                ).wait_recv()
+            send(
+                kt.at[half(c), cols], kt.at[half(c), cols], xsem.at[f], xrsem.at[f], partner, k
+            ).wait_recv()
 
         fwds[f].start()
 
@@ -583,13 +510,14 @@
             copy = send(
                 mixb.at[owned(part, peer), cols],
                 rbuf[part].at[i, :, cols],
-                rs.at[part, n, i],
-                rr.at[part, n, i],
+                rs.at[part, n],
+                rr.at[part, n],
                 p,
                 peer,
             )
             copy.start()
-            sends[part].append(copy)
+        every = rbuf[part].at[pl.ds(1, 7), :, cols]
+        sends[part].append(send(every, every, rs.at[part, n], rr.at[part, n], p, lax.rem(k + 1, 8)))
 
     def share_sums(part):
         row, rows = PARTS[part]
@@ -604,10 +532,11 @@
         for i in range(1, 8):
             peer = lax.rem(k + i, 8)
             copy = send(
-                mlp[part].at[peer], rml[part].at[i], rs.at[part, 3, i], rr.at[part, 3, i], p, peer
+                mlp[part].at[peer], rml[part].at[i], rs.at[part, 3], rr.at[part, 3], p, peer
             )
             copy.start()
-            sends[part].append(copy)
+        every = rml[part].at[pl.ds(1, 7)]
+        sends[part].append(send(every, every, rs.at[part, 3], rr.at[part, 3], p, lax.rem(k + 1, 8)))
 
     def merge(part):
         row, rows = PARTS[part]
@@ -640,10 +569,11 @@
         for i in range(1, 8):
             peer = lax.rem(k + i, 8)
             copy = send(
-                obuf[part], tout_h.at[owned(part, k)], gs.at[part, i], gr.at[part, i], p, peer
+                obuf[part], tout_h.at[owned(part, k)], gs.at[part], gr.at[part], p, peer
             )
             copy.start()
-            gathers[part].append(copy)
+        every = tout_h.at[pl.ds(row, 7 * piece)]
+        gathers[part].append(send(every, every, gs.at[part], gr.at[part], p, lax.rem(k + 1, 8)))
         return own
 
     for n in range(len(CHUNKS[0])):
@@ -657,29 +587,14 @@
     own_a.wait()
     own_b.wait()
     aout_copy.wait()
-    for part in range(2):
-        for i in range(1, 8):
-            src = lax.rem(k + 8 - i, 8)
-            send(
-                obuf[part], tout_h.at[owned(part, src)], gs.at[part, i], gr.at[part, i], p, src
-            ).wait_recv()
+    for copy in gathers[0] + gathers[1]:
+        copy.wait_recv()
     for copy in gathers[0] + gathers[1] + sends[0] + sends[1] + fwds:
         copy.wait_send()
 
-    @pl.when(outer)
-    def _():
-        for f in range(len(FEATURES)):
-            for i in (2, 4, 6):
-                directs[f][i - 1].wait_send()
-            hops[f].wait_send()
-            for copy in onward[f]:
-                copy.wait_send()
-
-    @pl.when(jnp.logical_not(outer))
-    def _():
-        for f in range(len(FEATURES)):
-            for copy in directs[f]:
-                copy.wait_send()
+    for f, col in enumerate(FEATURES):
+        seven = kt.at[pl.ds(0, 7 * PIECE), pl.ds(col, 256)]
+        send(seven, seven, xsem.at[f], xrsem.at[f], partner, k).wait_send()
 
     @pl.when(p < last)
     def _():
@@ -738,7 +653,6 @@
             vm((AR + TAIL, 128), BF16),
             vm((TR, AR + TAIL), BF16),
             vm((3, AR + TAIL, 256), BF16),
-            vm((PIECE, CT), BF16),
             vm((TR, CT), BF16),
             vm((TR, CT), BF16),
             vm((TR, CT), BF16),
@@ -762,17 +676,14 @@
             dma((3,)),
             dma((4,)),
             dma((4,)),
-            dma((3, 8)),
-            dma((3, 8)),
             dma((3,)),
             dma((3,)),
-            dma((3, 4)),
             dma((3,)),
             dma((3,)),
-            dma((2, 4, 8)),
-            dma((2, 4, 8)),
-            dma((2, 8)),
-            dma((2, 8)),
+            dma((2, 4)),
+            dma((2, 4)),
+            dma((2,)),
+            dma((2,)),
         ],
         compiler_params=pltpu.CompilerParams(
             collective_id=0, has_side_effects=True, vmem_limit_bytes=60 * 1024 * 1024

time: 73.7 us -> 72.3 us (0.981)
  Pallas kernels: 68.9 us -> 67.4 us
    pallas_call x1, Pallas kernels: 68.9 us -> 67.4 us  [body(): pl.pallas_call(kernel, out_shape=(jax.ShapeDtypeStruct((AR, 128), BF16),...]
where the time goes in v5:
time: 72.3 us; the launch traced here: 72.1 us
  Pallas kernels  67.4 us (93%)
  local copies, waits for them, and re-layouts  3.98 us (6%)
    pallas_call x1, Pallas kernels, body(): pl.pallas_call(kernel, out_shape=(jax.ShapeDtypeStruct((AR, 128), BF16),...  67.4 us
    unnamed x2, local copies, waits for them, and re-layouts  3.98 us

profile of v5, /device:TPU:0, one launch (start us, length us, event | category | flops | bytes accessed | tf_op | source)
XLA Modules:
  0.0 72.1 jit_solution(4372744901884088562)
XLA Ops:
  0.6 67.4 %shard_map.140 = (bf16[3072,128]{1,0:T(8,128)(2,1)}, bf16[384,768]{1,0:T(8,128)(2,1)}) custom-call(s32[96]{0:T(128)} %shift_ref.1, bf16[3072,128]{1,0:T(8,128)(2,1)} %atoms_h.1, f32[1,128]{1,0:T(1,128)} %bitcast.3, bf16[128,384]{1,0:T(8,128)(2,1)} %qkv_h.1, bf16[128,128]{1,0:T(8,128)(2,1)} %proj_h.1, bf16[4,3072,128]{2,1,0:T(8,128)(2,1)} %abias_h.1, ...), custom_call_target="tpu_custom_call" | custom-call | tf_op jit(solution)/shard_map/pallas_call | solution.py:628
  68.1 2.1 %copy.17 = bf16[3072,128]{1,0:T(8,128)(2,1)} copy(bf16[3072,128]{1,0:T(8,128)(2,1)} %get-tuple-element.4) | data formatting | bytes 1572864
  70.1 1.9 %copy.18 = bf16[384,768]{1,0:T(8,128)(2,1)} copy(bf16[384,768]{1,0:T(8,128)(2,1)} %get-tuple-element.5) | data formatting | bytes 1179648

commit v6 on v5

--- a/solution.py
+++ b/solution.py
@@ -72,6 +72,7 @@
     ao,
     hot,
     hid,
+    rly,
     kn,
     rep,
     nrm,
@@ -97,6 +98,9 @@
     hr,
     xsem,
     xrsem,
+    rls,
+    rlr,
+    rfs,
     fs,
     fr,
     rs,
@@ -109,6 +113,9 @@
     k = lax.axis_index("ka")
     c = lax.rem(p, 2)
     cp = lax.div(p, 2)
+    zh, zl = lax.rem(cp, 2), lax.rem(k, 2)
+    outer = zh == zl
+    cp_flip, k_flip, p_flip = cp + 1 - 2 * zh, k + 1 - 2 * zl, p + 2 - 4 * zh
     last = 15
     barrier = pltpu.get_barrier_semaphore()
 
@@ -148,11 +155,29 @@
     def direct(i):
         return lax.rem(cp + i, 8) * 2 + c
 
+    def relayed(x):
+        return (2 * x + zh) * 2 + c
+
     for i in range(1, 8):
         hello(p, lax.rem(k + i, 8))
-        hello(direct(i), cp)
-
-    @pl.when(k != cp)
+
+    @pl.when(outer)
+    def _():
+        for i in (2, 4, 6):
+            hello(direct(i), cp)
+        for x in range(4):
+            hello(relayed(x), cp_flip)
+        hello(p_flip, k_flip)
+
+    @pl.when(jnp.logical_not(outer))
+    def _():
+        for i in range(1, 8):
+            hello(direct(i), cp)
+        for y in range(4):
+            hello(2 * k_flip + c, 2 * y + 1 - zl)
+            hello(2 * k + c, 2 * y + 1 - zl)
+
+    @pl.when(jnp.logical_and(outer, k != cp))
     def _():
         for s in range(8):
             hello(2 * k + c, s)
@@ -278,6 +303,7 @@
         + jnp.where(p > 0, 1, 0)
         + jnp.where(p < last, 1, 0)
         + jnp.where(k != cp, 8, 0)
+        + jnp.where(outer, 1, 0)
     )
     pl.semaphore_wait(barrier, greeted)
     right = jnp.minimum(p + 1, last)
@@ -369,7 +395,8 @@
 
     def pooled_sends(f):
         cols = pl.ds(FEATURES[f], 256)
-        for i in range(1, 8):
+
+        def go(i):
             send(
                 rep.at[rows48(k), cols],
                 kt.at[landing(c, k), cols],
@@ -379,22 +406,52 @@
                 cp,
             ).start()
 
+        @pl.when(outer)
+        def _():
+            hop(f).start()
+            for i in (2, 4, 6):
+                go(i)
+
+        @pl.when(jnp.logical_not(outer))
+        def _():
+            for i in (1, 3, 5, 7, 2, 4, 6):
+                go(i)
+
+    def hop(f):
+        cols = pl.ds(FEATURES[f], 256)
+        return send(
+            rep.at[rows48(k), cols], rly.at[:, cols], rls.at[f], rlr.at[f], p_flip, k_flip
+        )
+
+    def pass_on(f):
+        cols = pl.ds(FEATURES[f], 256)
+
+        @pl.when(outer)
+        def _():
+            hop(f).wait_recv()
+            for x in range(4):
+                send(
+                    rly.at[:, cols],
+                    kt.at[landing(c, k_flip), cols],
+                    rfs.at[f],
+                    xrsem.at[f],
+                    relayed(x),
+                    cp_flip,
+                ).start()
+
     for f, col in enumerate(FEATURES):
         cols = pl.ds(col, 256)
 
         if f == 0:
             hidden(0, (0, 6, 7))
             pooled = mm(hot[:, 0:AR], hid[0, 0:AR, :])
-            hidden_three(1, 0, 2)
-            hidden(1, (6, 7))
+            hidden(1, (0, 1, 2))
             tail_rows()
             hidden(0, (8,))
-            hidden(1, (8,))
             counts = jnp.sum(mlb[...], axis=1, keepdims=True)
             pooled += mm(hot[:, AR : AR + TAIL], hid[0, AR : AR + TAIL, :])
         else:
-            if f == 2:
-                hidden_three(2, 0, 3)
+            hidden_three(f, 2 - f, 3)
             pooled = mm(hot[...], hid[f])
         rep[:, cols] = (pooled / counts).astype(BF16)
 
@@ -403,7 +460,10 @@
     tscale = 1.0 / math.sqrt(float(HD))
     copies["wq"].wait()
     nrm[...] = normed(rep[...].astype(F32), tgain[...].reshape(1, CT))
+    pass_on(0)
+    pass_on(1)
     qt[...] = (mm(nrm[...], wq[...]) * tscale).astype(BF16)
+    pass_on(2)
     partner = p + 1 - 2 * c
 
     @pl.when(k == cp)
@@ -593,8 +653,21 @@
         copy.wait_send()
 
     for f, col in enumerate(FEATURES):
-        seven = kt.at[pl.ds(0, 7 * PIECE), pl.ds(col, 256)]
-        send(seven, seven, xsem.at[f], xrsem.at[f], partner, k).wait_send()
+        cols = pl.ds(col, 256)
+
+        def sent(count, sem):
+            some = kt.at[pl.ds(0, count * PIECE), cols]
+            send(some, some, sem, xrsem.at[f], partner, k).wait_send()
+
+        @pl.when(outer)
+        def _():
+            hop(f).wait_send()
+            sent(3, xsem.at[f])
+            sent(4, rfs.at[f])
+
+        @pl.when(jnp.logical_not(outer))
+        def _():
+            sent(7, xsem.at[f])
 
     @pl.when(p < last)
     def _():
@@ -653,6 +726,7 @@
             vm((AR + TAIL, 128), BF16),
             vm((TR, AR + TAIL), BF16),
             vm((3, AR + TAIL, 256), BF16),
+            vm((PIECE, CT), BF16),
             vm((TR, CT), BF16),
             vm((TR, CT), BF16),
             vm((TR, CT), BF16),
@@ -680,6 +754,9 @@
             dma((3,)),
             dma((3,)),
             dma((3,)),
+            dma((3,)),
+            dma((3,)),
+            dma((3,)),
             dma((2, 4)),
             dma((2, 4)),
             dma((2,)),

time: 72.3 us -> 68.9 us (0.953)
  Pallas kernels: 67.4 us -> 64.1 us
    pallas_call x1, Pallas kernels: 67.4 us -> 64.1 us  [body(): pl.pallas_call(kernel, out_shape=(jax.ShapeDtypeStruct((AR, 128), BF16),...]
where the time goes in v6:
time: 68.9 us; the launch traced here: 68.7 us
  Pallas kernels  64.1 us (93%)
  local copies, waits for them, and re-layouts  3.98 us (6%)
    pallas_call x1, Pallas kernels, body(): pl.pallas_call(kernel, out_shape=(jax.ShapeDtypeStruct((AR, 128), BF16),...  64.1 us
    unnamed x2, local copies, waits for them, and re-layouts  3.98 us

profile of v6, /device:TPU:0, one launch (start us, length us, event | category | flops | bytes accessed | tf_op | source)
XLA Modules:
  0.0 68.7 jit_solution(696408086989884678)
XLA Ops:
  0.6 64.1 %shard_map.140 = (bf16[3072,128]{1,0:T(8,128)(2,1)}, bf16[384,768]{1,0:T(8,128)(2,1)}) custom-call(s32[96]{0:T(128)} %shift_ref.1, bf16[3072,128]{1,0:T(8,128)(2,1)} %atoms_h.1, f32[1,128]{1,0:T(1,128)} %bitcast.3, bf16[128,384]{1,0:T(8,128)(2,1)} %qkv_h.1, bf16[128,128]{1,0:T(8,128)(2,1)} %proj_h.1, bf16[4,3072,128]{2,1,0:T(8,128)(2,1)} %abias_h.1, ...), custom_call_target="tpu_custom_call" | custom-call | tf_op jit(solution)/shard_map/pallas_call | solution.py:701
  64.8 2.1 %copy.17 = bf16[3072,128]{1,0:T(8,128)(2,1)} copy(bf16[3072,128]{1,0:T(8,128)(2,1)} %get-tuple-element.4) | data formatting | bytes 1572864
  66.8 1.9 %copy.18 = bf16[384,768]{1,0:T(8,128)(2,1)} copy(bf16[384,768]{1,0:T(8,128)(2,1)} %get-tuple-element.5) | data formatting | bytes 1179648

commit v7 on v6

--- a/solution.py
+++ b/solution.py
@@ -680,6 +680,28 @@
         to_left.wait_send()
 
 
+def write_out(a_ref, t_ref, a_out, t_out, a_buf, t_buf, in_sem, out_sem):
+    moves = []
+    for n in range(2):
+        for m, (src, buf, dst, rows) in enumerate(
+            ((a_ref, a_buf, a_out, AR // 2), (t_ref, t_buf, t_out, TR // 2))
+        ):
+            r = pl.ds(n * rows, rows)
+            moves.append(
+                (
+                    pltpu.make_async_copy(src.at[r], buf.at[r], in_sem.at[n, m]),
+                    pltpu.make_async_copy(buf.at[r], dst.at[r], out_sem.at[n, m]),
+                )
+            )
+    for fetch, _ in moves:
+        fetch.start()
+    for fetch, put in moves:
+        fetch.wait()
+        put.start()
+    for _, put in moves:
+        put.wait()
+
+
 def body(
     atoms,
     atom_gain,
@@ -698,12 +720,13 @@
     hbm = pl.BlockSpec(memory_space=pl.ANY)
     vm = pltpu.VMEM
     dma = pltpu.SemaphoreType.DMA
-    return pl.pallas_call(
+    shapes = (
+        jax.ShapeDtypeStruct((AR, 128), BF16),
+        jax.ShapeDtypeStruct((TR, CT), BF16),
+    )
+    aout, tout = pl.pallas_call(
         kernel,
-        out_shape=(
-            jax.ShapeDtypeStruct((AR, 128), BF16),
-            jax.ShapeDtypeStruct((TR, CT), BF16),
-        ),
+        out_shape=shapes,
         in_specs=[pl.BlockSpec(memory_space=pltpu.SMEM)] + [hbm] * 12,
         out_specs=(hbm, hbm),
         scratch_shapes=[
@@ -780,6 +803,13 @@
         token_o,
         pair_bias,
     )
+    return pl.pallas_call(
+        write_out,
+        out_shape=shapes,
+        in_specs=[hbm, hbm],
+        out_specs=(hbm, hbm),
+        scratch_shapes=[vm((AR, 128), BF16), vm((TR, CT), BF16), dma((2, 2)), dma((2, 2))],
+    )(aout, tout)
 
 
 def solution(mesh):

time: 68.9 us -> 67.2 us (0.975)
  local copies, waits for them, and re-layouts: 3.98 us -> 0 us
  Pallas kernels: 64.1 us -> 66.2 us
    unnamed x2 -> x0, local copies, waits for them, and re-layouts: 3.98 us -> none
    pallas_call x1 -> x2, Pallas kernels: 64.1 us -> 66.2 us  [the longest x1 64.1 us: body(): pl.pallas_call(kernel, out_shape=shapes, in_specs=[pl.BlockSpec(memory_sp...]
where the time goes in v7:
time: 67.2 us; the launch traced here: 67 us
  Pallas kernels  66.2 us (99%)
  between operations  0.8 us (1%)
    pallas_call x1, Pallas kernels, body(): pl.pallas_call(kernel, out_shape=shapes, in_specs=[pl.BlockSpec(memory_sp...  64.1 us
    pallas_call x1, Pallas kernels, body(): pl.pallas_call(write_out, out_shape=shapes, in_specs=[hbm, hbm], out_spec...  2.13 us

profile of v7, /device:TPU:0, one launch (start us, length us, event | category | flops | bytes accessed | tf_op | source)
XLA Modules:
  0.0 67.0 jit_solution(473947592674382091)
XLA Ops:
  0.6 64.1 %shard_map.140 = (bf16[3072,128]{1,0:T(8,128)(2,1)}, bf16[384,768]{1,0:T(8,128)(2,1)}) custom-call(s32[96]{0:T(128)} %shift_ref.1, bf16[3072,128]{1,0:T(8,128)(2,1)} %atoms_h.1, f32[1,128]{1,0:T(1,128)} %bitcast.3, bf16[128,384]{1,0:T(8,128)(2,1)} %qkv_h.1, bf16[128,128]{1,0:T(8,128)(2,1)} %proj_h.1, bf16[4,3072,128]{2,1,0:T(8,128)(2,1)} %abias_h.1, ...), custom_call_target="tpu_custom_call" | custom-call | tf_op jit(solution)/shard_map/pallas_call | solution.py:727
  64.7 2.1 %shard_map.141 = (bf16[3072,128]{1,0:T(8,128)(2,1)}, bf16[384,768]{1,0:T(8,128)(2,1)}) custom-call(bf16[3072,128]{1,0:T(8,128)(2,1)} %get-tuple-element.4.a_ref, bf16[384,768]{1,0:T(8,128)(2,1)} %get-tuple-element.5.t_ref), custom_call_target="tpu_custom_call" | custom-call | tf_op jit(solution)/shard_map/pallas_call | solution.py:806
